TPU v7x, 32 devices: a whole 2x2x4 slice. The times are simulated.
32 devices in a mesh: dp: 4 (over y, core), fsdp: 8 (over z, x).
Axes of the slice: x: 2, y: 2, z: 4, core: 2. Of those that a mesh axis runs over, the one named last changes fastest.
Arguments:
- cells: bfloat16 [32768, 1024], P(('dp', 'fsdp')), may hold values from -6 to 6
- segment_ids: int32 [32, 1024], P(('dp', 'fsdp')), may hold values from 0 to 7, never falling along the last dimension, each value on 1 to 256 neighbouring positions
- valid: int32 [32, 1024], P(('dp', 'fsdp')), may hold values 0 or 1
- norm1_gain: bfloat16 [1024], P(('dp', 'fsdp')), may hold values from 0.5 to 1.5
- norm1_bias: bfloat16 [1024], P(('dp', 'fsdp')), may hold values from -3 to 3
- qkv_weight: bfloat16 [1024, 3072], P(('dp', 'fsdp')), may hold values from -0.1875 to 0.1875
- qv_bias: bfloat16 [2048], P(('dp', 'fsdp')), may hold values from -1 to 1
- out_weight: bfloat16 [1024, 1024], P(('dp', 'fsdp')), may hold values from -0.75 to 0.75
- out_bias: bfloat16 [1024], P(('dp', 'fsdp')), may hold values from -3 to 3
- norm2_gain: bfloat16 [1024], P(('dp', 'fsdp')), may hold values from 0.5 to 1.5
- norm2_bias: bfloat16 [1024], P(('dp', 'fsdp')), may hold values from -3 to 3
- up_weight: bfloat16 [1024, 4096], P(('dp', 'fsdp')), may hold values from -0.1875 to 0.1875
- up_bias: bfloat16 [4096], P(('dp', 'fsdp')), may hold values from -3 to 3
- down_weight: bfloat16 [4096, 1024], P(('dp', 'fsdp')), may hold values from -0.125 to 0.125
- down_bias: bfloat16 [1024], P(('dp', 'fsdp')), may hold values from -3 to 3
- out_grad: bfloat16 [32768, 1024], P(('dp', 'fsdp')), may hold values from -6 to 6
Outputs:
- out_cells: bfloat16 [32768, 1024], P(('dp', 'fsdp'))
- cells_grad: bfloat16 [32768, 1024], P(('dp', 'fsdp'))
- norm1_gain_grad: float32 [1024], P(('dp', 'fsdp'))
- norm1_bias_grad: float32 [1024], P(('dp', 'fsdp'))
- qkv_weight_grad: float32 [1024, 3072], P(('dp', 'fsdp'))
- qv_bias_grad: float32 [2048], P(('dp', 'fsdp'))
- out_weight_grad: float32 [1024, 1024], P(('dp', 'fsdp'))
- out_bias_grad: float32 [1024], P(('dp', 'fsdp'))
- norm2_gain_grad: float32 [1024], P(('dp', 'fsdp'))
- norm2_bias_grad: float32 [1024], P(('dp', 'fsdp'))
- up_weight_grad: float32 [1024, 4096], P(('dp', 'fsdp'))
- up_bias_grad: float32 [4096], P(('dp', 'fsdp'))
- down_weight_grad: float32 [4096, 1024], P(('dp', 'fsdp'))
- down_bias_grad: float32 [1024], P(('dp', 'fsdp'))
Inputs may be any that keep to these rules, and one draw needn't show every extreme that they name: `segment_ids`: along each row the slide numbers never fall; each slide covers 1 to 256 consecutive cells. `valid`: 1 marks a real cell, 0 padding, anywhere in a row.
All inputs are finite; a program needn't handle non-finite values. No bound on the sum of `valid` on one device may be relied on, other than what follows from the above.
Results may differ from a plain program's by a relative error of at most 0.013.
Values may be sent and summed in bfloat16 or wider, within the bound.
No kernel may reach another device: no remote copies, remote signals or barrier semaphores. Data moves between devices by JAX's collectives and lax.ppermute only.
A program may use at most 256 MiB of HBM per device.

v0:
```python
from functools import partial
import itertools
import math

import jax
import jax.numpy as jnp
from jax import lax
from jax.experimental import pallas as pl
from jax.experimental.pallas import tpu as pltpu
from jax.sharding import Mesh, PartitionSpec as P

HEADS = 16
HEAD = 64
EPSILON = 1e-05
SCALE = 1.0 / math.sqrt(HEAD)
AXES = ("y", "core", "zh", "zl", "x")
NN = (((1,), (0,)), ((), ()))
NT = (((1,), (1,)), ((), ()))
TN = (((0,), (0,)), ((), ()))
LANES = 128
QUERIES = 128
REACH = 256
MASKED = -1e30
VMEM_LIMIT = 60 * 1024 * 1024
ANY = pl.BlockSpec(memory_space=pl.ANY)
SMEM = pl.BlockSpec(memory_space=pltpu.SMEM)


def dot(left, right, dims=NN):
    return lax.dot_general(left, right, dims, preferred_element_type=jnp.float32)


def params(limit=VMEM_LIMIT):
    return pltpu.CompilerParams(vmem_limit_bytes=limit)


def cost(flops, moved, special=0):
    return pl.CostEstimate(
        flops=int(flops) // 16, bytes_accessed=int(moved) // 16, transcendentals=int(special) // 16
    )


class Grid:
    def __init__(self, sizes):
        self.sizes = dict(zip(AXES, sizes))
        self.total = math.prod(sizes)

    def coords(self):
        return {name: lax.axis_index(name) for name in AXES}

    def block(self, coords):
        place = 0
        for name in AXES:
            place = place * self.sizes[name] + coords[name]
        return place


    def offsets(self, names):
        spans = [range(self.sizes[name]) for name in names]
        return [dict(zip(names, steps)) for steps in itertools.product(*spans) if any(steps)]

    def send(self, value, step):
        names = tuple(step)
        sizes = [self.sizes[name] for name in names]
        pairs = []
        for place in itertools.product(*[range(size) for size in sizes]):
            target = [(at + step[name]) % size for at, name, size in zip(place, names, sizes)]
            pairs.append((flat(place, sizes), flat(target, sizes)))
        return lax.ppermute(value, names, pairs)


def flat(place, sizes):
    index = 0
    for at, size in zip(place, sizes):
        index = index * size + at
    return index


def behind(grid, coords, step):
    return grid.block(
        {
            name: lax.rem(coords[name] + grid.sizes[name] - step.get(name, 0), grid.sizes[name])
            for name in AXES
        }
    )


hold = lax.optimization_barrier


def gather_near(grid, own, rounds=(("zh", "zl"),)):
    held = own[None]
    for names in rounds:
        arrived = [grid.send(held, step) for step in grid.offsets(names)]
        held = jnp.concatenate([held] + arrived, 0)
    return held


def gather_plane(grid, line):
    return [line] + [grid.send(line, step) for step in grid.offsets(("y", "x"))]


def gather_core(grid, lines):
    return [grid.send(piece, {"core": 1}) for piece in lines]


def gather_places(grid, coords, rounds=(("zh", "zl"),)):
    lines = [{}] + grid.offsets(("y", "x"))
    steps = lines + [{**line, "core": 1} for line in lines]
    near = [{}]
    for names in rounds:
        near = [{**step, **deep} for deep in [{}] + grid.offsets(names) for step in near]
    return jnp.stack(
        [behind(grid, coords, {**step, **deep}) for step in steps for deep in near]
    ).astype(jnp.int32)


class Gathered:
    def __init__(self, groups):
        rows = groups[0][0][0].shape[1]
        if rows % 16:
            columns = []
            for pieces, places, _, _ in groups:
                blocks = jnp.concatenate(pieces, 0)
                placed = jnp.zeros_like(blocks).at[places].set(blocks)
                columns.append(placed.reshape(-1, blocks.shape[2]))
            groups = [whole_group(jnp.concatenate(columns, 1))]
        self.pieces = [piece for group in groups for piece in group[0]]
        self.places = jnp.concatenate([group[1] for group in groups])
        self.layout = [
            ([piece.shape for piece in pieces], begin, end) for pieces, _, begin, end in groups
        ]

    @property
    def count(self):
        return len(self.pieces)


def whole_group(array):
    return [array[None]], jnp.zeros((1,), jnp.int32), 0, array.shape[1]


def row_copies(layout, places, pieces, first, target, width, sem):
    copies, number, at = [], 0, 0
    for shapes, begin, end in layout:
        low, high = max(first, begin), min(first + width, end)
        for blocks, rows, _ in shapes:
            for slot in range(blocks):
                if low < high:
                    start = pl.multiple_of(places[number] * rows, rows)
                    copies.append(
                        pltpu.make_async_copy(
                            pieces[at].at[slot, :, pl.ds(low - begin, high - low)],
                            target.at[pl.ds(start, rows), pl.ds(low - first, high - low)],
                            sem,
                        )
                    )
                number += 1
            at += 1
    return copies


def add_up(terms):
    return sum(term.astype(jnp.float32) for term in terms)


class Term:
    def __init__(self, array, axes, places=()):
        self.array, self.axes, self.places = array, axes, dict(places)

    def at(self, places):
        return Term(self.array, self.axes, {**self.places, **places})

    def value(self):
        axes, chosen, tail = self.axes, self.places, list(self.array.shape[len(self.axes) :])
        starts = [chosen.get(name, 0) for name in axes] + [0] * len(tail)
        sizes = dict(zip(axes, self.array.shape))
        shape = [1 if name in chosen else sizes[name] for name in axes]
        block = lax.dynamic_slice(self.array, starts, shape + tail)
        return block.reshape([sizes[name] for name in axes if name not in chosen] + tail)


class Scatter:
    plane = ("y", "x")

    def __init__(self, grid, coords, arrays, axes):
        self.grid, self.coords = grid, coords
        self.terms = [Term(array, axes) for array in arrays]
        self.steps = grid.offsets(self.plane)

    def sends(self, wire=jnp.bfloat16):
        self.sent = []
        for step in self.steps:
            target = {
                name: lax.rem(self.coords[name] + step[name], self.grid.sizes[name])
                for name in self.plane
            }
            self.sent.append(add_up(term.at(target).value() for term in self.terms).astype(wire))
        return self.sent

    def move(self, token):
        arrived = [self.grid.send(value, step) for value, step in zip(self.sent, self.steps)]
        arrived = hold((arrived, token))[0]
        own = {name: self.coords[name] for name in self.plane}
        self.terms = [term.at(own) for term in self.terms]
        axes = tuple(axis for axis in self.terms[0].axes if axis not in own)
        self.terms += [Term(value, axes) for value in arrived]
        return arrived

    def blocks(self, wire=jnp.bfloat16):
        axes = [axis for axis in self.terms[0].axes if axis not in self.terms[0].places]
        lead = [axes.index(name) for name in ("zh", "zl")]
        value = add_up(jnp.moveaxis(term.value(), lead, (0, 1)) for term in self.terms)
        self.left = value.astype(wire).reshape(-1, *value.shape[2:])
        return self.left

    def along_z(self):
        rows = self.left.reshape(-1, self.left.shape[-1])
        own = lax.psum_scatter(rows, ("zh", "zl"), scatter_dimension=0, tiled=True)
        return own.astype(jnp.float32).reshape(self.left.shape[1:])


def scatter_small(grid, coords, array, rounds):
    terms = [Term(array, AXES)]
    for names in rounds:
        steps = grid.offsets(names)
        sent = [
            add_up(
                term.at(
                    {name: lax.rem(coords[name] + step[name], grid.sizes[name]) for name in names}
                ).value()
                for term in terms
            )
            for step in steps
        ]
        arrived = [grid.send(value, step) for value, step in zip(sent, steps)]
        terms = [term.at({name: coords[name] for name in names}) for term in terms]
        axes = tuple(axis for axis in AXES if axis not in terms[0].places)
        terms += [Term(value, axes) for value in arrived]
    return add_up(term.value() for term in terms)


def center_rows(rows):
    mean = jnp.mean(rows, axis=-1, keepdims=True)
    centred = rows - mean
    rate = lax.rsqrt(jnp.mean(centred * centred, axis=-1, keepdims=True) + EPSILON)
    return centred * rate, rate


def norm_pull(unit, rate, gain, cots):
    scaled = cots * gain
    return rate * (
        scaled
        - jnp.mean(scaled, axis=-1, keepdims=True)
        - unit * jnp.mean(scaled * unit, axis=-1, keepdims=True)
    )


def column_sum(values):
    return jnp.sum(values, axis=0, keepdims=True)


def gelu_parts(values):
    phi = 0.5 + 0.5 * lax.erf(values * (1.0 / math.sqrt(2.0)))
    bell = jnp.exp(values * values * -0.5) * (1.0 / math.sqrt(2.0 * math.pi))
    return values * phi, phi + values * bell


def key_range(first, rows):
    return max(0, first - REACH), min(rows, first + QUERIES + REACH)


def pair_rows(block, low):
    zero = jnp.zeros_like(block)
    return jnp.concatenate([jnp.where(low, block, zero), jnp.where(low, zero, block)], 0)


def twice(block, axis):
    return jnp.concatenate([block, block], axis)


def attend_kernel(layout, counts, places, *refs):
    pieces, refs = refs[: counts[0]], refs[counts[0] + counts[1] :]
    cells, gain, shift, shift_qkv, ids_col, ids_row, live_row, refs = *refs[:7], refs[7:]
    normed, qkv, mixed, log_sums, weight, bias, sem = refs
    rows, width = cells.shape
    span = qkv.shape[2]
    step = pl.program_id(0)
    copies = row_copies(layout, places, pieces, 0, weight, 3 * width, sem)

    @pl.when(step == 0)
    def _():
        for copy in copies:
            copy.start()

        @pl.loop(0, rows // 256)
        def _(part):
            here = pl.ds(pl.multiple_of(part * 256, 256), 256)
            unit, _ = center_rows(cells[here, :].astype(jnp.float32))
            normed[here, :] = (unit * gain[...] + shift[...]).astype(jnp.bfloat16)

        for block, first in enumerate(range(0, rows, QUERIES)):
            start, stop = key_range(first, rows)
            shape = (QUERIES, stop - start)
            same = ids_col[first : first + QUERIES, :] == ids_row[:, start:stop]
            query_at = lax.broadcasted_iota(jnp.int32, shape, 0) + first
            key_at = lax.broadcasted_iota(jnp.int32, shape, 1) + start
            allowed = same & ((live_row[:, start:stop] == 1) | (query_at == key_at))
            bias[block, :, 0 : stop - start] = jnp.where(allowed, 0.0, MASKED)
        for copy in copies:
            copy.wait()

    @pl.when(step >= 0)
    def _():
        for part in range(3):
            here = pl.ds(pl.multiple_of(part * width + step * span, span), span)
            product = dot(normed[...], weight[:, here]) + shift_qkv[:, here]
            qkv[part] = product.astype(jnp.bfloat16)

    low = lax.broadcasted_iota(jnp.int32, (QUERIES, LANES), 1) < HEAD
    for pair in range(span // LANES):
        lanes = slice(pair * LANES, (pair + 1) * LANES)
        for block, first in enumerate(range(0, rows, QUERIES)):
            start, stop = key_range(first, rows)
            here = slice(first, first + QUERIES)
            query = pair_rows(qkv[0, here, lanes] * jnp.bfloat16(SCALE), low)
            scores = dot(query, qkv[1, start:stop, lanes], NT)
            scores = scores + twice(bias[block, :, 0 : stop - start], 0)
            top = jnp.max(scores, axis=1, keepdims=True)
            expd = jnp.exp(scores - top)
            total = jnp.sum(expd, axis=1, keepdims=True)
            out = dot(expd.astype(jnp.bfloat16), qkv[2, start:stop, lanes]) / total
            mixed[here, lanes] = jnp.where(low, out[:QUERIES], out[QUERIES:]).astype(jnp.bfloat16)
            spread = jnp.broadcast_to(top + jnp.log(total), (2 * QUERIES, LANES)).T[0:1]
            log_sums[pair, 0:1, here] = spread[:, :QUERIES]
            log_sums[pair, 1:2, here] = spread[:, QUERIES:]


def attend(qkv_all, cells, gain, shift, shift_qkv, ids, live, after=(), pairs=2):
    rows, width = cells.shape
    span = pairs * LANES
    row = pl.BlockSpec((1, rows), lambda h: (0, 0))
    vector = pl.BlockSpec((1, width), lambda h: (0, 0))
    whole = pl.BlockSpec((rows, width), lambda h: (0, 0))
    low, full, struct = jnp.bfloat16, jnp.float32, jax.ShapeDtypeStruct
    return pl.pallas_call(
        partial(attend_kernel, qkv_all.layout, (qkv_all.count, len(after))),
        grid=(width // span,),
        in_specs=[SMEM]
        + [ANY] * (qkv_all.count + len(after))
        + [
            whole,
            vector,
            vector,
            pl.BlockSpec((1, 3 * width), lambda h: (0, 0)),
            pl.BlockSpec((rows, 1), lambda h: (0, 0)),
            row,
            row,
        ],
        out_specs=[
            whole,
            pl.BlockSpec((3, rows, span), lambda h: (0, 0, h)),
            pl.BlockSpec((rows, span), lambda h: (0, h)),
            pl.BlockSpec((pairs, 2, rows), lambda h: (h, 0, 0)),
        ],
        out_shape=[
            struct((rows, width), low),
            struct((3, rows, width), low),
            struct((rows, width), low),
            struct((width // LANES, 2, rows), full),
        ],
        scratch_shapes=[
            pltpu.VMEM((width, 3 * width), low),
            pltpu.VMEM((rows // QUERIES, QUERIES, QUERIES + 2 * REACH), full),
            pltpu.SemaphoreType.DMA,
        ],
        compiler_params=params(),
        cost_estimate=cost(30 * 10**9, 18 * rows * width, 10**7),
        name="attend",
    )(
        qkv_all.places,
        *qkv_all.pieces,
        *after,
        cells,
        gain.reshape(1, -1),
        shift.reshape(1, -1),
        shift_qkv.reshape(1, -1),
        ids.reshape(rows, 1),
        ids,
        live,
    )


def attend_back_kernel(
    outer, count, core, ids_col, ids_row, live_col, qkv, log_sums, d_mixed, *refs
):
    lefts, refs = refs[: 2 * outer], refs[2 * outer + count :]
    d_qkv, sums, sent, kept, bias, d_key, d_value, turned, cots, query_sum = refs
    pair = pl.program_id(0)
    rows = qkv.shape[1]

    @pl.when(pair == 0)
    def _():
        for place, left in enumerate(lefts):
            block = left.shape[1]
            turned[place * block : (place + 1) * block, :] = left[...].T
        for block, first in enumerate(range(0, rows, QUERIES)):
            start, stop = key_range(first, rows)
            shape = (stop - start, QUERIES)
            same = ids_col[start:stop, :] == ids_row[:, first : first + QUERIES]
            query_at = lax.broadcasted_iota(jnp.int32, shape, 1) + first
            key_at = lax.broadcasted_iota(jnp.int32, shape, 0) + start
            allowed = same & ((live_col[start:stop, :] == 1) | (query_at == key_at))
            bias[block, 0 : stop - start, :] = jnp.where(allowed, 0.0, MASKED)

    d_key[...] = jnp.zeros_like(d_key)
    d_value[...] = jnp.zeros_like(d_value)
    low = lax.broadcasted_iota(jnp.int32, (QUERIES, LANES), 1) < HEAD
    query_sum[...] = jnp.zeros_like(query_sum)

    @pl.when(pair >= 0)
    def _():
        for block, first in enumerate(range(0, rows, QUERIES)):
            start, stop = key_range(first, rows)
            here = slice(first, first + QUERIES)
            query = pair_rows(qkv[0, here, :] * jnp.bfloat16(SCALE), low)
            cot = pair_rows(d_mixed[here, :], low)
            keys, values = qkv[1, start:stop, :], qkv[2, start:stop, :]
            scores = dot(keys, query, NT) + twice(bias[block, 0 : stop - start, :], 1)
            ends = jnp.concatenate([log_sums[0, 0:1, here], log_sums[0, 1:2, here]], 1)
            probs = jnp.exp(scores - ends)
            weighted = probs * dot(values, cot, NT)
            d_scores = (weighted - probs * column_sum(weighted)).astype(jnp.bfloat16)
            d_value[start:stop, :] += dot(probs.astype(jnp.bfloat16), cot)
            d_key[start:stop, :] += dot(d_scores, query)
            both = dot(d_scores, keys, TN)
            d_query = (jnp.where(low, both[:QUERIES], both[QUERIES:]) * SCALE).astype(jnp.bfloat16)
            d_qkv[0, here, :] = d_query
            query_sum[...] += column_sum(d_query.astype(jnp.float32))

    d_qkv[1] = d_key[...].astype(jnp.bfloat16)
    value_low = d_value[...].astype(jnp.bfloat16)
    d_qkv[2] = value_low
    odd = lax.rem(pair, 2)
    width = 2 * LANES
    for part in range(3):
        side = pl.ds(pl.multiple_of(part * width + odd * LANES, LANES), LANES)
        cots[:, side] = d_qkv[part]

    @pl.when(odd == 1)
    def _():
        half = turned.shape[0] // 2
        for out, first in ((sent, 0), (kept, half)):

            for begin in range(0, half, 256):
                side = slice(first + begin, first + begin + 256)
                grads = dot(turned[side, :], cots[...]).astype(jnp.bfloat16)
                for part in range(3):
                    out[part, begin : begin + 256, :] = grads[:, part * width : (part + 1) * width]

    sums[0:1, :] = query_sum[...]
    sums[1:2, :] = column_sum(value_low.astype(jnp.float32))


def attend_back(core, outer, ids, live, qkv, log_sums, d_mixed, normed, after=()):
    _, rows, width = qkv.shape
    pairs = width // LANES
    per_outer = normed.shape[1] // (2 * outer)
    column = pl.BlockSpec((rows, 1), lambda h, c: (0, 0))
    triple = pl.BlockSpec((3, rows, LANES), lambda h, c: (0, 0, h))
    grads = pl.BlockSpec((3, outer * per_outer, 2 * LANES), lambda h, c: (0, 0, h // 2))
    low, full, struct = jnp.bfloat16, jnp.float32, jax.ShapeDtypeStruct
    lefts = [
        pl.BlockSpec((rows, per_outer), lambda h, c, y=y: (0, y * 2 + 1 - c[0]))
        for y in range(outer)
    ] + [
        pl.BlockSpec((rows, per_outer), lambda h, c, y=y: (0, y * 2 + c[0])) for y in range(outer)
    ]
    grad_struct = struct((3, outer * per_outer, width), low)
    return pl.pallas_call(
        partial(attend_back_kernel, outer, len(after)),
        grid_spec=pltpu.PrefetchScalarGridSpec(
            num_scalar_prefetch=1,
            grid=(pairs,),
            in_specs=[
                column,
                pl.BlockSpec((1, rows), lambda h, c: (0, 0)),
                column,
                triple,
                pl.BlockSpec((1, 2, rows), lambda h, c: (h, 0, 0)),
                pl.BlockSpec((rows, LANES), lambda h, c: (0, h)),
            ]
            + lefts
            + [ANY] * len(after),
            out_specs=[triple, pl.BlockSpec((2, LANES), lambda h, c: (0, h)), grads, grads],
            scratch_shapes=[
                pltpu.VMEM((rows // QUERIES, QUERIES + 2 * REACH, QUERIES), full),
                pltpu.VMEM((rows, LANES), full),
                pltpu.VMEM((rows, LANES), full),
                pltpu.VMEM((2 * outer * per_outer, rows), low),
                pltpu.VMEM((rows, 6 * LANES), low),
                pltpu.VMEM((1, LANES), full),
            ],
        ),
        out_shape=[struct(qkv.shape, low), struct((2, width), full), grad_struct, grad_struct],
        compiler_params=params(),
        cost_estimate=cost(44 * 10**9, 28 * rows * width, 10**7),
        name="attend_back",
    )(
        core.reshape(1),
        ids.reshape(rows, 1),
        ids,
        live.reshape(rows, 1),
        qkv,
        log_sums,
        d_mixed,
        *[normed] * (2 * outer),
        *after,
    )


def feed_up_kernel(layout, counts, chunk, places, *refs):
    pieces, refs = refs[: counts[0]], refs[counts[0] + counts[1] :]
    mixed, cells, vectors, up_bias, inner, normed, hidden, slopes = refs[:8]
    w_out, w_up, sem_out, sem_up = refs[8:]
    width, wide = w_up.shape
    out_copies = row_copies(layout, places, pieces, wide, w_out, width, sem_out)
    up_copies = row_copies(layout, places, pieces, 0, w_up, wide, sem_up)
    opening = pl.program_id(0) == 0

    @pl.when(opening)
    def _():
        for copy in out_copies + up_copies:
            copy.start()
        for copy in out_copies:
            copy.wait()

    stream = cells[...].astype(jnp.float32) + dot(mixed[...], w_out[...]) + vectors[2:3, :]
    inner[...] = stream
    unit, _ = center_rows(stream)
    rows = (unit * vectors[0:1, :] + vectors[1:2, :]).astype(jnp.bfloat16)
    normed[...] = rows

    @pl.when(opening)
    def _():
        for copy in up_copies:
            copy.wait()

    for first in range(0, wide, chunk):
        here = slice(first, first + chunk)
        value, slope = gelu_parts(dot(rows, w_up[:, here]) + up_bias[:, here])
        hidden[:, here] = value.astype(jnp.bfloat16)
        slopes[:, here] = slope.astype(jnp.bfloat16)


def feed_up(up_out, mixed, cells, vectors, up_bias, after=(), block=256, chunk=512):
    rows, width = cells.shape
    wide = up_bias.shape[0]
    narrow = pl.BlockSpec((block, width), lambda i: (i, 0))
    broad = pl.BlockSpec((block, wide), lambda i: (i, 0))
    low, struct = jnp.bfloat16, jax.ShapeDtypeStruct
    return pl.pallas_call(
        partial(feed_up_kernel, up_out.layout, (up_out.count, len(after)), chunk),
        grid=(rows // block,),
        in_specs=[SMEM]
        + [ANY] * (up_out.count + len(after))
        + [
            narrow,
            narrow,
            pl.BlockSpec((4, width), lambda i: (0, 0)),
            pl.BlockSpec((1, wide), lambda i: (0, 0)),
        ],
        out_specs=[narrow, narrow, broad, broad],
        out_shape=[
            struct((rows, width), jnp.float32),
            struct((rows, width), low),
            struct((rows, wide), low),
            struct((rows, wide), low),
        ],
        scratch_shapes=[
            pltpu.VMEM((width, width), low),
            pltpu.VMEM((width, wide), low),
            pltpu.SemaphoreType.DMA,
            pltpu.SemaphoreType.DMA,
        ],
        compiler_params=params(),
        cost_estimate=cost(2 * rows * width * (wide + width), 32 * 2**20, 10**7),
        name="feed_up",
    )(up_out.places, *up_out.pieces, *after, mixed, cells, vectors, up_bias.reshape(1, -1))


def feed_down_kernel(layouts, counts, chunk, places_up, places_down, *refs):
    pieces_up, refs = refs[: counts[0]], refs[counts[0] :]
    pieces_down, refs = refs[: counts[1]], refs[counts[1] + counts[2] :]
    inner, slopes, out_grad, vectors = refs[:4]
    d_up, d_inner, e_rows, d_mixed, sums, up_sums = refs[4:10]
    w_out, w_up, w_down, sem_out, sem_up, sem_down = refs[10:]
    width, wide = w_up.shape
    out_copies = row_copies(layouts[0], places_up, pieces_up, wide, w_out, width, sem_out)
    up_copies = row_copies(layouts[0], places_up, pieces_up, 0, w_up, wide, sem_up)
    down_copies = row_copies(layouts[1], places_down, pieces_down, 0, w_down, width, sem_down)
    opening = pl.program_id(0) == 0

    @pl.when(opening)
    def _():
        for copy in down_copies + up_copies + out_copies:
            copy.start()
        sums[...] = jnp.zeros_like(sums)
        up_sums[...] = jnp.zeros_like(up_sums)
        for copy in down_copies:
            copy.wait()

    cot = out_grad[...]
    for first in range(0, wide, chunk):
        here = slice(first, first + chunk)
        back = dot(cot, w_down[here, :], NT) * slopes[:, here].astype(jnp.float32)
        slope = back.astype(jnp.bfloat16)
        d_up[:, here] = slope
        up_sums[:, here] += column_sum(slope.astype(jnp.float32))

    @pl.when(opening)
    def _():
        for copy in up_copies + out_copies:
            copy.wait()

    d_two = dot(d_up[...], w_up[...], NT)
    unit, rate = center_rows(inner[...])
    cot_wide = cot.astype(jnp.float32)
    pulled = cot_wide + norm_pull(unit, rate, vectors[0:1, :], d_two)
    d_inner[...] = pulled
    low = pulled.astype(jnp.bfloat16)
    e_rows[...] = low
    d_mixed[...] = dot(low, w_out[...], NT).astype(jnp.bfloat16)
    sums[0:1, :] += column_sum(d_two * unit)
    sums[1:2, :] += column_sum(d_two)
    sums[2:3, :] += column_sum(low.astype(jnp.float32))
    sums[3:4, :] += column_sum(cot_wide)


def feed_down(up_out, down, inner, slopes, out_grad, vectors, after=(), block=256, chunk=512):
    rows, width = inner.shape
    wide = slopes.shape[1]
    narrow = pl.BlockSpec((block, width), lambda i: (i, 0))
    broad = pl.BlockSpec((block, wide), lambda i: (i, 0))
    low, full, struct = jnp.bfloat16, jnp.float32, jax.ShapeDtypeStruct
    return pl.pallas_call(
        partial(
            feed_down_kernel,
            (up_out.layout, down.layout),
            (up_out.count, down.count, len(after)),
            chunk,
        ),
        grid=(rows // block,),
        in_specs=[SMEM, SMEM]
        + [ANY] * (up_out.count + down.count + len(after))
        + [narrow, broad, narrow, pl.BlockSpec((4, width), lambda i: (0, 0))],
        out_specs=[
            broad,
            narrow,
            narrow,
            narrow,
            pl.BlockSpec((4, width), lambda i: (0, 0)),
            pl.BlockSpec((1, wide), lambda i: (0, 0)),
        ],
        out_shape=[
            struct((rows, wide), low),
            struct((rows, width), full),
            struct((rows, width), low),
            struct((rows, width), low),
            struct((4, width), full),
            struct((1, wide), full),
        ],
        scratch_shapes=[
            pltpu.VMEM((width, width), low),
            pltpu.VMEM((width, wide), low),
            pltpu.VMEM((wide, width), low),
            pltpu.SemaphoreType.DMA,
            pltpu.SemaphoreType.DMA,
            pltpu.SemaphoreType.DMA,
        ],
        compiler_params=params(),
        cost_estimate=cost(2 * rows * width * (2 * wide + width), 48 * 2**20, 0),
        name="feed_down",
    )(
        up_out.places,
        down.places,
        *up_out.pieces,
        *down.pieces,
        *after,
        inner,
        slopes,
        out_grad,
        vectors,
    )


def output_kernel(layout, counts, places, *refs):
    pieces, refs = refs[: counts[0]], refs[counts[0] + counts[1] :]
    inner, hidden, shift, out_cells, weight, sem = refs
    copies = row_copies(layout, places, pieces, 0, weight, weight.shape[1], sem)

    @pl.when(pl.program_id(0) == 0)
    def _():
        for copy in copies:
            copy.start()
        for copy in copies:
            copy.wait()

    layer_out = inner[...] + dot(hidden[...], weight[...]) + shift[...]
    out_cells[...] = layer_out.astype(jnp.bfloat16)


def output(down, inner, hidden, shift, after=(), block=256):
    rows, width = inner.shape
    wide = hidden.shape[1]
    narrow = pl.BlockSpec((block, width), lambda i: (i, 0))
    return pl.pallas_call(
        partial(output_kernel, down.layout, (down.count, len(after))),
        grid=(rows // block,),
        in_specs=[SMEM]
        + [ANY] * (down.count + len(after))
        + [
            narrow,
            pl.BlockSpec((block, wide), lambda i: (i, 0)),
            pl.BlockSpec((1, width), lambda i: (0, 0)),
        ],
        out_specs=narrow,
        out_shape=jax.ShapeDtypeStruct((rows, width), jnp.bfloat16),
        scratch_shapes=[pltpu.VMEM((wide, width), jnp.bfloat16), pltpu.SemaphoreType.DMA],
        compiler_params=params(),
        cost_estimate=cost(2 * rows * width * wide, 24 * 2**20, 0),
        name="output",
    )(down.places, *down.pieces, *after, inner, hidden, shift.reshape(1, -1))


def grad_kernel(outer, ends, core, *refs):
    lefts, refs = refs[: outer * len(ends)], refs[outer * len(ends) :]
    rights, out, mark, turned = refs[: len(ends)], refs[-3], refs[-2], refs[-1]
    mark[...] = jnp.zeros_like(mark)
    chunk_at = pl.program_id(1)
    begin = 0
    for pair, end in enumerate(ends):

        @pl.when(chunk_at == begin)
        def _(pair=pair):
            for y in range(outer):
                left = lefts[pair * outer + y][...]
                turned[y * left.shape[1] : (y + 1) * left.shape[1], :] = left.T

        @pl.when((chunk_at >= begin) & (chunk_at < end))
        def _(pair=pair):
            cots = rights[pair][...].reshape(rights[pair].shape[-2:])
            out[...] = dot(turned[...], cots).astype(out.dtype).reshape(out.shape)

        begin = end


def half_grad(core, outer, pairs, after=(), block=256, chunk=1024):
    rows, width = pairs[0][0].shape
    per_outer = width // (2 * outer)
    block = min(block, per_outer)
    steps = per_outer // block
    ends, lefts, left_specs, right_specs, begin = [], [], [], [], 0
    for left, right, first, span in pairs:
        count, depth = span // chunk, right.shape[-1] // chunk
        for y in range(outer):
            lefts.append(left)
            left_specs.append(
                pl.BlockSpec(
                    (rows, block), lambda m, n, c, y=y: (0, (y * 2 + c[0]) * steps + m)
                )
            )

        def pick(n, begin=begin, count=count, first=first):
            return first // chunk + jnp.clip(n - begin, 0, count - 1)

        if right.ndim == 3:
            right_specs.append(
                pl.BlockSpec(
                    (1, rows, chunk),
                    lambda m, n, c, pick=pick, depth=depth: (pick(n) // depth, 0, pick(n) % depth),
                )
            )
        else:
            right_specs.append(
                pl.BlockSpec((rows, chunk), lambda m, n, c, pick=pick: (0, pick(n)))
            )
        begin += count
        ends.append(begin)
    total = begin * chunk

    def body(core, *refs):
        grad_kernel(outer, ends, core, *refs[: -3 - len(after)], *refs[-3:])

    return pl.pallas_call(
        body,
        grid_spec=pltpu.PrefetchScalarGridSpec(
            num_scalar_prefetch=1,
            grid=(steps, begin),
            in_specs=left_specs + right_specs + [ANY] * len(after),
            out_specs=[
                pl.BlockSpec((outer, block, chunk), lambda m, n, c: (0, m, n)),
                pl.BlockSpec((8, LANES), lambda m, n, c: (0, 0)),
            ],
            scratch_shapes=[pltpu.VMEM((outer * block, rows), jnp.bfloat16)],
        ),
        out_shape=[
            jax.ShapeDtypeStruct((outer, per_outer, total), jnp.bfloat16),
            jax.ShapeDtypeStruct((8, LANES), jnp.float32),
        ],
        compiler_params=params(),
        cost_estimate=cost(rows * width * total, rows * (width + 2 * total) + width * total),
        name="half_grad",
    )(core.reshape(1), *lefts, *[pair[1] for pair in pairs], *after)


def cells_kernel(layout, counts, places, *refs):
    pieces, refs = refs[: counts[0]], refs[counts[0] + counts[1] :]
    d_qkv, cells, d_inner, gain, cells_grad, sums, weight, sem = refs
    width = cells.shape[1]
    copies = row_copies(layout, places, pieces, 0, weight, 3 * width, sem)
    opening = pl.program_id(0) == 0

    @pl.when(opening)
    def _():
        for copy in copies:
            copy.start()
        sums[...] = jnp.zeros_like(sums)

    unit, rate = center_rows(cells[...].astype(jnp.float32))

    @pl.when(opening)
    def _():
        for copy in copies:
            copy.wait()

    d_one = sum(
        dot(d_qkv[part], weight[:, pl.ds(part * width, width)], NT) for part in range(3)
    )
    cells_grad[...] = (d_inner[...] + norm_pull(unit, rate, gain[...], d_one)).astype(jnp.bfloat16)
    sums[0:1, :] += column_sum(d_one * unit)
    sums[1:2, :] += column_sum(d_one)


def cells_back(qkv_all, d_qkv, cells, d_inner, gain, after=(), block=256):
    rows, width = cells.shape
    narrow = pl.BlockSpec((block, width), lambda i: (i, 0))
    return pl.pallas_call(
        partial(cells_kernel, qkv_all.layout, (qkv_all.count, len(after))),
        grid=(rows // block,),
        in_specs=[SMEM]
        + [ANY] * (qkv_all.count + len(after))
        + [
            pl.BlockSpec((3, block, width), lambda i: (0, i, 0)),
            narrow,
            narrow,
            pl.BlockSpec((1, width), lambda i: (0, 0)),
        ],
        out_specs=[narrow, pl.BlockSpec((2, width), lambda i: (0, 0))],
        out_shape=[
            jax.ShapeDtypeStruct((rows, width), jnp.bfloat16),
            jax.ShapeDtypeStruct((2, width), jnp.float32),
        ],
        scratch_shapes=[pltpu.VMEM((width, 3 * width), jnp.bfloat16), pltpu.SemaphoreType.DMA],
        compiler_params=params(),
        cost_estimate=cost(6 * rows * width * width, 14 * rows * width + 6 * width * width),
        name="cells_back",
    )(
        qkv_all.places,
        *qkv_all.pieces,
        *after,
        d_qkv,
        cells,
        d_inner,
        gain.reshape(1, -1),
    )


def local(
    grid,
    cells,
    segment_ids,
    valid,
    norm1_gain,
    norm1_bias,
    qkv_weight,
    qv_bias,
    out_weight,
    out_bias,
    norm2_gain,
    norm2_bias,
    up_weight,
    up_bias,
    down_weight,
    down_bias,
    out_grad,
):
    width = cells.shape[1]
    wide = up_weight.shape[1]
    coords = grid.coords()
    own_rows = qkv_weight.shape[0]
    places = gather_places(grid, coords)
    vectors = (
        norm1_gain,
        norm1_bias,
        qv_bias,
        out_bias,
        norm2_gain,
        norm2_bias,
        up_bias,
        down_bias,
    )
    groups = -(-len(vectors) // own_rows)
    packed = jnp.stack([jnp.pad(vector, (0, LANES - vector.shape[0])) for vector in vectors])
    packed = jnp.pad(packed, ((0, groups * own_rows - len(vectors)), (0, 0)))
    packed = packed.reshape(own_rows, groups * LANES)

    joined = lax.all_gather(
        jnp.concatenate([up_weight, out_weight], 1), AXES, axis=0, tiled=True
    )
    up_out = Gathered([whole_group(joined)])
    line = gather_near(grid, jnp.concatenate([qkv_weight, packed], 1))
    near = gather_plane(grid, line)
    qkv_pieces = near + gather_core(grid, near)
    qkv_all = Gathered([(qkv_pieces, places, 0, line.shape[2])])
    down_own, _ = hold((down_weight, near))
    down_all = lax.all_gather(down_own, AXES, axis=0, tiled=True)
    down_all = Gathered([whole_group(down_all)])

    arrived = jnp.concatenate([piece[:, :, 3 * width :] for piece in qkv_pieces], 0)
    arrived = arrived.reshape(grid.total, groups * own_rows, LANES)[:, : len(vectors)]
    arrived = jnp.zeros_like(arrived).at[places].set(arrived)
    unpacked = [
        arrived[:, at, : vector.shape[0]].reshape(-1).astype(jnp.float32)
        for at, vector in enumerate(vectors)
    ]
    gain_one, shift_one, b_qv, b_out, gain_two, shift_two, b_up, b_down = unpacked
    rows_two = jnp.stack([gain_two, shift_two, b_out, b_down])

    qkv_bias = jnp.concatenate([b_qv[:width], jnp.zeros_like(b_out), b_qv[width:]])
    normed, qkv, mixed, log_sums = attend(
        qkv_all, cells, gain_one, shift_one, qkv_bias, segment_ids, valid
    )
    inner, normed_two, hidden, slopes = feed_up(up_out, mixed, cells, rows_two, b_up)

    mine, other = coords["core"], 1 - coords["core"]
    outer = grid.sizes["y"]
    block_axes = ("y", "zh", "zl", "x")
    block_sizes = [grid.sizes[name] for name in block_axes]

    def shared(product):
        return product.reshape(block_sizes + [-1, product.shape[-1]])

    def start(pairs, after=()):
        sent, mark = half_grad(other, outer, pairs, after)
        return mark, grid.send(sent, {"core": 1})

    def under_way(kept, arrived):
        return Scatter(grid, coords, [shared(kept), shared(arrived)], block_axes)

    down_pairs = [(hidden, out_grad, 0, width)]
    down_mark, down_core = start(down_pairs)
    down_kept, _ = half_grad(mine, outer, down_pairs, [down_mark])
    down_sum = under_way(down_kept, down_core)
    d_up, d_inner, e_rows, d_mixed, sums, up_sums = feed_down(
        up_out, down_all, inner, slopes, out_grad, rows_two, down_sum.sends()
    )
    up_pairs = [(normed_two, d_up, 0, wide), (mixed, e_rows, 0, width)]
    down_sum.move(sums)
    up_mark, up_core = start(up_pairs, [down_sum.blocks()])
    down_total = down_sum.along_z()
    up_kept, _ = half_grad(mine, outer, up_pairs, [up_mark])
    up_sum = under_way(up_kept, up_core)
    d_qkv, qv_sums, qkv_sent, qkv_kept = attend_back(
        mine,
        outer,
        segment_ids,
        valid,
        qkv,
        log_sums,
        d_mixed,
        normed,
        up_sum.sends() + [down_total],
    )
    qkv_core = grid.send(qkv_sent, {"core": 1})
    qkv_sum = Scatter(
        grid,
        coords,
        [term.reshape([3] + block_sizes + [-1, width]) for term in (qkv_kept, qkv_core)],
        ("part",) + block_axes,
    )
    qkv_sends = qkv_sum.sends()
    up_moved = up_sum.move((qv_sums, qkv_sends[-1][:, 0, 0, :8, :LANES]))
    cells_grad, one_sums = cells_back(
        qkv_all, d_qkv, cells, d_inner, gain_one, qkv_sends + up_moved
    )
    up_blocks = up_sum.blocks()
    up_total = up_sum.along_z()
    out_cells = output(down_all, inner, hidden, b_down, [one_sums, up_blocks])
    ahead = qkv_sum.move(out_cells)
    qkv_sum.blocks()
    qkv_total = qkv_sum.along_z()

    vector_grads = (
        one_sums[0],
        one_sums[1],
        qv_sums,
        sums[2],
        sums[0],
        sums[1],
        up_sums,
        sums[3],
    )
    sizes = [grid.sizes[name] for name in AXES]
    stacked = jnp.concatenate([grad.reshape(*sizes, -1) for grad in vector_grads], -1)
    summed = scatter_small(
        grid, coords, stacked, (("core",), ("y", "x"), ("zl",), ("zh",))
    )
    parts, first = [], 0
    for vector in vectors:
        parts.append(summed[first : first + vector.shape[0]])
        first += vector.shape[0]
    return (
        out_cells,
        cells_grad,
        parts[0],
        parts[1],
        jnp.concatenate([qkv_total[part] for part in range(3)], 1),
        parts[2],
        up_total[:, wide:],
        parts[3],
        parts[4],
        parts[5],
        up_total[:, :wide],
        parts[6],
        down_total,
        parts[7],
    )


def solution(mesh):
    outer, inner_size = mesh.devices.shape
    sizes = (outer // 2, 2, inner_size // 4, 2, 2)
    fine = Mesh(mesh.devices.reshape(sizes), AXES)
    rows, vector = P(AXES, None), P(AXES)
    return jax.shard_map(
        partial(local, Grid(sizes)),
        mesh=fine,
        in_specs=(
            rows,
            rows,
            rows,
            vector,
            vector,
            rows,
            vector,
            rows,
            vector,
            vector,
            vector,
            rows,
            vector,
            rows,
            vector,
            rows,
        ),
        out_specs=(
            rows,
            rows,
            vector,
            vector,
            rows,
            vector,
            rows,
            vector,
            vector,
            vector,
            rows,
            vector,
            rows,
            vector,
        ),
        check_vma=False,
    )
```

profile of v0, /device:TPU:0, one launch (start us, length us, event | category | flops | bytes accessed | tf_op | source)
XLA Modules:
  0.0 425.9 jit_solution(5256838647091626483)
XLA Ops:
  13.4 3.1 collective-permute-start
  16.5 2.6 collective-permute-start.1
  19.1 6.1 %collective-permute-done = bf16[1,32,3200]{2,1,0:T(8,128)(2,1)S(1)} collective-permute-done((bf16[1,32,3200]{2,1,0:T(8,128)(2,1)S(1)}, bf16[1,32,3200]{2,1,0:T(8,128)(2,1)S(1)}, u32[]{:S(2)}, u32[]{:S(2)}) %collective-permute-start) | collective-permute-done | bytes 204832 | tf_op jit(solution)/shard_map/ppermute | solution.py:69
  25.2 12.2 %collective-permute-done.1 = bf16[1,32,3200]{2,1,0:T(8,128)(2,1)S(1)} collective-permute-done((bf16[1,32,3200]{2,1,0:T(8,128)(2,1)S(1)}, bf16[1,32,3200]{2,1,0:T(8,128)(2,1)S(1)}, u32[]{:S(2)}, u32[]{:S(2)}) %collective-permute-start.1) | collective-permute-done | bytes 204832 | tf_op jit(solution)/shard_map/ppermute | solution.py:69
  41.0 25.3 %collective-permute-done.3.refs_1_ = bf16[4,32,3200]{2,1,0:T(8,128)(2,1)S(1)} collective-permute-done((bf16[4,32,3200]{2,1,0:T(8,128)(2,1)S(1)}, bf16[4,32,3200]{2,1,0:T(8,128)(2,1)S(1)}, u32[]{:S(2)}, u32[]{:S(2)}) %collective-permute-start.3) | collective-permute-done | bytes 819232 | tf_op jit(solution)/shard_map/ppermute | solution.py:69
  66.3 16.6 %collective-permute-done.5.refs_3_ = bf16[4,32,3200]{2,1,0:T(8,128)(2,1)S(1)} collective-permute-done((bf16[4,32,3200]{2,1,0:T(8,128)(2,1)S(1)}, bf16[4,32,3200]{2,1,0:T(8,128)(2,1)S(1)}, u32[]{:S(2)}, u32[]{:S(2)}) %collective-permute-start.5) | collective-permute-done | bytes 819232 | tf_op jit(solution)/shard_map/ppermute | solution.py:69
  96.8 38.3 %attend.1 = (bf16[1024,1024]{1,0:T(8,128)(2,1)}, bf16[3,1024,1024]{2,1,0:T(8,128)(2,1)}, bf16[1024,1024]{1,0:T(8,128)(2,1)}, f32[8,2,1024]{2,1,0:T(2,128)}) custom-call(s32[32]{0:T(128)} %stack.240.places, bf16[4,32,3200]{2,1,0:T(8,128)(2,1)} %copy-done, bf16[4,32,3200]{2,1,0:T(8,128)(2,1)} %copy-done.6, bf16[4,32,3200]{2,1,0:T(8,128)(2,1)} %copy-done.7, ...), custom_call_target="tpu_custom_call" | custom-call | flops 1875000064 | bytes 1179648 | tf_op jit(solution)/shard_map/attend/pallas_call | solution.py:346
  135.7 26.9 %feed_up.1 = (f32[1024,1024]{1,0:T(8,128)}, bf16[1024,1024]{1,0:T(8,128)(2,1)}, bf16[1024,4096]{1,0:T(8,128)(2,1)}, bf16[1024,4096]{1,0:T(8,128)(2,1)}) custom-call(s32[1]{0:T(128)} %constant.67.clone.1.places.places_up.places_down, bf16[1,1024,5120]{2,1,0:T(8,128)(2,1)} %bitcast.231, bf16[1024,1024]{1,0:T(8,128)(2,1)} %get-tuple-element.53.refs_1_.refs_2_.refs_3_, ...), custom_call_target="tpu_custom_call" | custom-call | flops 671088640 | bytes 2097152 | tf_op jit(solution)/shard_map/feed_up/pallas_call | solution.py:562
  162.7 8.5 %half_grad.4 = (bf16[2,1024,1024]{2,1,0:T(8,128)(2,1)}, f32[8,128]{1,0:T(8,128)}) custom-call(s32[1]{0:T(128)} %bitcast.81.core, bf16[1024,4096]{1,0:T(8,128)(2,1)} %get-tuple-element.54.refs_0_.refs_1_.refs_4_, bf16[1024,4096]{1,0:T(8,128)(2,1)} %get-tuple-element.54.refs_0_.refs_1_.refs_4_, bf16[1024,1024]{1,0:T(8,128)(2,1)} %refs_7_.1), custom_call_target="tpu_custom_call" | custom-call | flops 268435456 | bytes 655360 | tf_op jit(solution)/shard_map/half_grad/pallas_call | solution.py:795
  171.4 9.1 %half_grad.5 = (bf16[2,1024,1024]{2,1,0:T(8,128)(2,1)}, f32[8,128]{1,0:T(8,128)}) custom-call(s32[1]{0:T(128)} %bitcast.42.core, bf16[1024,4096]{1,0:T(8,128)(2,1)} %get-tuple-element.54.refs_0_.refs_1_.refs_4_, bf16[1024,4096]{1,0:T(8,128)(2,1)} %get-tuple-element.54.refs_0_.refs_1_.refs_4_, bf16[1024,1024]{1,0:T(8,128)(2,1)} %refs_7_.1, ...), custom_call_target="tpu_custom_call" | custom-call | flops 268435456 | bytes 655360 | tf_op jit(solution)/shard_map/half_grad/pallas_call | solution.py:795
  181.5 4.7 %fusion.14 = (bf16[2,2,128,1024]{3,2,1,0:T(8,128)(2,1)S(1)}, bf16[2,2,128,1024]{3,2,1,0:T(8,128)(2,1)S(1)}, bf16[2,2,128,1024]{3,2,1,0:T(8,128)(2,1)S(1)}) fusion(bf16[2,2,2,2,128,1024]{5,4,3,2,1,0:T(8,128)(2,1)} %bitcast.83, s32[]{:T(128)S(6)} %select_n.36, s32[]{:T(128)S(6)} %select_n.35, bf16[2,2,2,2,128,1024]{5,4,3,2,1,0:T(8,128)(2,1)} %bitcast.241, ...), kind=kLoop, calls=%fused_computation.27 | loop fusion | flops 6291456 | bytes 9437200 | tf_op jit(solution)/shard_map/convert_element_type | solution.py:198
  187.7 2.0 collective-permute-start.13
  189.7 12.3 %all-gather.3.cloned.1.call-done = bf16[4096,1024]{1,0:T(8,128)(2,1)} async-done(((bf16[128,1024]{1,0:T(8,128)(2,1)}), bf16[4096,1024]{1,0:T(8,128)(2,1)}) %all-gather.3.cloned.1.call-update) | async-done | bytes 8388624 | tf_op jit(solution)/shard_map/all_gather | solution.py:927
  202.1 31.7 %feed_down.1 = (bf16[1024,4096]{1,0:T(8,128)(2,1)}, f32[1024,1024]{1,0:T(8,128)}, bf16[1024,1024]{1,0:T(8,128)(2,1)}, bf16[1024,1024]{1,0:T(8,128)(2,1)}, f32[4,1024]{1,0:T(4,128)}, /*index=5*/f32[1,4096]{1,0:T(1,128)}) custom-call(s32[1]{0:T(128)} %constant.67.clone.1.places.places_up.places_down, s32[1]{0:T(128)} %constant.67.clone.1.places.places_up.places_down, ...), custom_call_target="tpu_custom_call" | custom-call | flops 1207959552 | bytes 3145728 | tf_op jit(solution)/shard_map/feed_down/pallas_call | solution.py:646
  235.5 4.6 %fusion.5 = bf16[2,2,128,1024]{3,2,1,0:T(8,128)(2,1)} fusion(bf16[2,2,128,1024]{3,2,1,0:T(8,128)(2,1)} %collective-permute-done.13, bf16[2,2,128,1024]{3,2,1,0:T(8,128)(2,1)} %collective-permute-done.12, bf16[2,2,128,1024]{3,2,1,0:T(8,128)(2,1)} %collective-permute-done.11, bf16[2,2,2,2,128,1024]{5,4,3,2,1,0:T(8,128)(2,1)} %bitcast.83, s32[]{:T(128)S(6)} %select_n.38, ...), kind=kLoop, calls=%fused_computation.11 | loop fusion | flops 5242880 | bytes 6291464 | tf_op jit(solution)/shard_map/convert_element_type | solution.py:214
  240.1 11.9 %half_grad.6 = (bf16[2,256,5120]{2,1,0:T(8,128)(2,1)}, f32[8,128]{1,0:T(8,128)}) custom-call(s32[1]{0:T(128)} %bitcast.81.core, bf16[1024,1024]{1,0:T(8,128)(2,1)} %get-tuple-element.62.refs_0_.refs_1_, bf16[1024,1024]{1,0:T(8,128)(2,1)} %get-tuple-element.62.refs_0_.refs_1_, bf16[1024,1024]{1,0:T(8,128)(2,1)} %get-tuple-element.53.refs_1_.refs_2_.refs_3_, ...), custom_call_target="tpu_custom_call" | custom-call | flops 335544320 | bytes 1048576 | tf_op jit(solution)/shard_map/half_grad/pallas_call | solution.py:795
  252.1 12.1 %half_grad.7 = (bf16[2,256,5120]{2,1,0:T(8,128)(2,1)}, f32[8,128]{1,0:T(8,128)}) custom-call(s32[1]{0:T(128)} %bitcast.42.core, bf16[1024,1024]{1,0:T(8,128)(2,1)} %get-tuple-element.62.refs_0_.refs_1_, bf16[1024,1024]{1,0:T(8,128)(2,1)} %get-tuple-element.62.refs_0_.refs_1_, bf16[1024,1024]{1,0:T(8,128)(2,1)} %get-tuple-element.53.refs_1_.refs_2_.refs_3_, ...), custom_call_target="tpu_custom_call" | custom-call | flops 335544320 | bytes 1048576 | tf_op jit(solution)/shard_map/half_grad/pallas_call | solution.py:795
  264.3 6.1 %fusion.11 = (bf16[2,2,32,5120]{3,2,1,0:T(8,128)(2,1)}, bf16[2,2,32,5120]{3,2,1,0:T(8,128)(2,1)}, bf16[2,2,32,5120]{3,2,1,0:T(8,128)(2,1)}) fusion(bf16[2,2,2,2,32,5120]{5,4,3,2,1,0:T(8,128)(2,1)} %bitcast.90, s32[]{:T(128)S(6)} %select_n.36, s32[]{:T(128)S(6)} %select_n.35, bf16[2,2,2,2,32,5120]{5,4,3,2,1,0:T(8,128)(2,1)} %bitcast.239, s32[]{:T(128)S(6)} %select_n.37, ...), kind=kLoop, calls=%fused_computation.24 | loop fusion | flops 7864320 | bytes 11796496 | tf_op jit(solution)/shard_map/convert_element_type | solution.py:198
  271.5 2.3 collective-permute-start.18
  274.9 16.9 %reduce-scatter.4.cloned.1.call-done = bf16[128,1024]{1,0:T(8,128)(2,1)} async-done(((bf16[512,1024]{1,0:T(8,128)(2,1)}), bf16[128,1024]{1,0:T(8,128)(2,1)}) %reduce-scatter.4.cloned.1.call-update) | async-done | bytes 262160 | tf_op jit(solution)/shard_map/reduce_scatter | solution.py:219
  291.8 1.8 convert_element_type.344.refs_7_
  293.6 50.5 %attend_back.1 = (bf16[3,1024,1024]{2,1,0:T(8,128)(2,1)}, f32[2,1024]{1,0:T(2,128)}, bf16[3,512,1024]{2,1,0:T(8,128)(2,1)}, bf16[3,512,1024]{2,1,0:T(8,128)(2,1)}) custom-call(s32[1]{0:T(128)} %bitcast.42.core, s32[1024,1]{1,0:T(8,128)} %copy.45.refs_12_.ids_col, s32[1,1024]{1,0:T(1,128)} %ids_row.1, s32[1024,1]{1,0:T(8,128)} %copy.46.live_col, ...), custom_call_target="tpu_custom_call" | custom-call | flops 2750000128 | bytes 1835008 | tf_op jit(solution)/shard_map/attend_back/pallas_call | solution.py:480
  344.2 5.1 %fusion.2 = bf16[2,2,32,5120]{3,2,1,0:T(8,128)(2,1)} fusion(bf16[2,2,32,5120]{3,2,1,0:T(8,128)(2,1)} %collective-permute-done.18.refs_13_, bf16[2,2,32,5120]{3,2,1,0:T(8,128)(2,1)S(1)} %collective-permute-done.17.refs_12_, bf16[2,2,32,5120]{3,2,1,0:T(8,128)(2,1)S(1)} %collective-permute-done.16.refs_11_, bf16[2,2,2,2,32,5120]{5,4,3,2,1,0:T(8,128)(2,1)} %bitcast.90, ...), kind=kLoop, calls=%fused_computation.4 | loop fusion | flops 6553600 | bytes 7864328 | tf_op jit(solution)/shard_map/convert_element_type | solution.py:214
  350.2 3.5 fusion.17
  357.3 15.5 %cells_back.1 = (bf16[1024,1024]{1,0:T(8,128)(2,1)}, f32[2,1024]{1,0:T(2,128)}) custom-call(s32[32]{0:T(128)} %stack.240.places, bf16[4,32,3200]{2,1,0:T(8,128)(2,1)} %copy-done, bf16[4,32,3200]{2,1,0:T(8,128)(2,1)} %copy-done.6, bf16[4,32,3200]{2,1,0:T(8,128)(2,1)} %copy-done.7, bf16[4,32,3200]{2,1,0:T(8,128)(2,1)} %copy-done.8, ...), custom_call_target="tpu_custom_call" | custom-call | flops 402653184 | bytes 1310720 | tf_op jit(solution)/shard_map/cells_back/pallas_call | solution.py:848
  374.2 15.8 %output.1 = bf16[1024,1024]{1,0:T(8,128)(2,1)} custom-call(s32[1]{0:T(128)} %constant.67.clone.1.places.places_up.places_down, bf16[1,4096,1024]{2,1,0:T(8,128)(2,1)} %bitcast.234, f32[2,1024]{1,0:T(2,128)} %get-tuple-element.80.refs_1_, bf16[4,32,5120]{2,1,0:T(8,128)(2,1)} %bitcast.236, f32[1024,1024]{1,0:T(8,128)} %get-tuple-element.58.refs_5_.refs_3_, ...), custom_call_target="tpu_custom_call" | custom-call | flops 536870912 | bytes 1572864 | tf_op jit(solution)/shard_map/output/pallas_call | solution.py:717
  393.1 2.7 fusion.18
  397.4 4.0 collective-permute-done.22
  401.7 3.5 collective-permute-done.23
  406.2 3.5 collective-permute-done.24
  411.5 1.8 slice.187
  414.8 2.4 reduce-scatter.6.cloned.1.call-done
  (177 shorter events, 47.4 us)
Async XLA Ops:
  7.2 128.6 %all-gather.5.cloned.1.call-start = ((), (), s32[]{:S(2)}) async-start(), calls=%async_computation.4 | async-start | bytes 10813440 | tf_op jit(solution)/shard_map/all_gather | solution.py:918
  9.0 193.1 %all-gather.3.cloned.1.call-start = ((), (), s32[]{:S(2)}) async-start(), calls=%async_computation.3 | async-start | bytes 8650752 | tf_op jit(solution)/shard_map/all_gather | solution.py:927
  13.4 11.8 %collective-permute-start = (bf16[1,32,3200]{2,1,0:T(8,128)(2,1)S(1)}, bf16[1,32,3200]{2,1,0:T(8,128)(2,1)S(1)}, u32[]{:S(2)}, u32[]{:S(2)}) collective-permute-start(bf16[1,32,3200]{2,1,0:T(8,128)(2,1)S(1)} %fusion.21), channel_id=1, source_target_pairs={{0,2},{2,0},{4,6},{6,4},{1,3},{3,1},{5,7},{7,5},{8,10},{10,8},{12,... | collective-permute-start | bytes 614408 | tf_op jit(solution)/shard_map/ppermute | solution.py:69
  16.5 20.9 %collective-permute-start.1 = (bf16[1,32,3200]{2,1,0:T(8,128)(2,1)S(1)}, bf16[1,32,3200]{2,1,0:T(8,128)(2,1)S(1)}, u32[]{:S(2)}, u32[]{:S(2)}) collective-permute-start(bf16[1,32,3200]{2,1,0:T(8,128)(2,1)S(1)} %fusion.21), channel_id=1, source_target_pairs={{0,4},{2,6},{4,0},{6,2},{1,5},{3,7},{5,1},{7,3},{8,12},{10,14},{12... | collective-permute-start | bytes 614408 | tf_op jit(solution)/shard_map/ppermute | solution.py:69
  19.0 18.3 %collective-permute-start.2 = (bf16[1,32,3200]{2,1,0:T(8,128)(2,1)S(1)}, bf16[1,32,3200]{2,1,0:T(8,128)(2,1)S(1)}, u32[]{:S(2)}, u32[]{:S(2)}) collective-permute-start(bf16[1,32,3200]{2,1,0:T(8,128)(2,1)S(1)} %fusion.21), channel_id=1, source_target_pairs={{0,6},{2,4},{4,2},{6,0},{1,7},{3,5},{5,3},{7,1},{8,14},{10,12},{12... | collective-permute-start | bytes 614408 | tf_op jit(solution)/shard_map/ppermute | solution.py:69
  37.5 28.8 %collective-permute-start.3 = (bf16[4,32,3200]{2,1,0:T(8,128)(2,1)S(1)}, bf16[4,32,3200]{2,1,0:T(8,128)(2,1)S(1)}, u32[]{:S(2)}, u32[]{:S(2)}) collective-permute-start(bf16[4,32,3200]{2,1,0:T(8,128)(2,1)S(1)} %pad_maximum_fusion.refs_0_), channel_id=1, source_target_pairs={{0,1},{1,0},{16,17},{17,16},{2,3},{3,2},{18,19},{19,18},{4,5},{5,4... | collective-permute-start | bytes 2457608 | tf_op jit(solution)/shard_map/ppermute | solution.py:69
  39.0 27.3 %collective-permute-start.4 = (bf16[4,32,3200]{2,1,0:T(8,128)(2,1)S(1)}, bf16[4,32,3200]{2,1,0:T(8,128)(2,1)S(1)}, u32[]{:S(2)}, u32[]{:S(2)}) collective-permute-start(bf16[4,32,3200]{2,1,0:T(8,128)(2,1)S(1)} %pad_maximum_fusion.refs_0_), channel_id=1, source_target_pairs={{0,16},{1,17},{16,0},{17,1},{2,18},{3,19},{18,2},{19,3},{4,20},{5,... | collective-permute-start | bytes 2457608 | tf_op jit(solution)/shard_map/ppermute | solution.py:69
  40.5 42.4 %collective-permute-start.5 = (bf16[4,32,3200]{2,1,0:T(8,128)(2,1)S(1)}, bf16[4,32,3200]{2,1,0:T(8,128)(2,1)S(1)}, u32[]{:S(2)}, u32[]{:S(2)}) collective-permute-start(bf16[4,32,3200]{2,1,0:T(8,128)(2,1)S(1)} %pad_maximum_fusion.refs_0_), channel_id=1, source_target_pairs={{0,17},{1,16},{16,1},{17,0},{2,19},{3,18},{18,3},{19,2},{4,21},{5,... | collective-permute-start | bytes 2457608 | tf_op jit(solution)/shard_map/ppermute | solution.py:69
  82.9 208.8 %reduce-scatter.4.cloned.1.call-start = ((), (), s32[]{:S(2)}) async-start(), calls=%async_computation.5 | async-start | bytes 1310720 | tf_op jit(solution)/shard_map/reduce_scatter | solution.py:219
  85.0 3.6 collective-permute-start.7
  85.5 4.3 %collective-permute-start.8 = (bf16[4,32,3200]{2,1,0:T(8,128)(2,1)S(1)}, bf16[4,32,3200]{2,1,0:T(8,128)(2,1)S(1)}, u32[]{:S(2)}, u32[]{:S(2)}) collective-permute-start(bf16[4,32,3200]{2,1,0:T(8,128)(2,1)S(1)} %collective-permute-done.4.refs_2_), channel_id=1, source_target_pairs={{0,8},{8,0},{1,9},{9,1},{2,10},{10,2},{3,11},{11,3},{4,12},{12,4},... | collective-permute-start | bytes 2457608 | tf_op jit(solution)/shard_map/ppermute | solution.py:69
  85.5 5.4 %collective-permute-start.9 = (bf16[4,32,3200]{2,1,0:T(8,128)(2,1)S(1)}, bf16[4,32,3200]{2,1,0:T(8,128)(2,1)S(1)}, u32[]{:S(2)}, u32[]{:S(2)}) collective-permute-start(bf16[4,32,3200]{2,1,0:T(8,128)(2,1)S(1)} %collective-permute-done.5.refs_3_), channel_id=1, source_target_pairs={{0,8},{8,0},{1,9},{9,1},{2,10},{10,2},{3,11},{11,3},{4,12},{12,4},... | collective-permute-start | bytes 2457608 | tf_op jit(solution)/shard_map/ppermute | solution.py:69
  171.2 10.3 %collective-permute-start.10 = (bf16[2,1024,1024]{2,1,0:T(8,128)(2,1)}, bf16[2,1024,1024]{2,1,0:T(8,128)(2,1)}, u32[]{:S(2)}, u32[]{:S(2)}) collective-permute-start(bf16[2,1024,1024]{2,1,0:T(8,128)(2,1)} %get-tuple-element.57), channel_id=1, source_target_pairs={{0,8},{8,0},{1,9},{9,1},{2,10},{10,2},{3,11},{11,3},{4,12},{12,4},... | collective-permute-start | bytes 12582920 | tf_op jit(solution)/shard_map/ppermute | solution.py:69
  186.2 47.7 %collective-permute-start.11 = (bf16[2,2,128,1024]{3,2,1,0:T(8,128)(2,1)S(1)}, bf16[2,2,128,1024]{3,2,1,0:T(8,128)(2,1)}, u32[]{:S(2)}, u32[]{:S(2)}) collective-permute-start(bf16[2,2,128,1024]{3,2,1,0:T(8,128)(2,1)S(1)} %get-tuple-element.117.refs_2_), channel_id=1, source_target_pairs={{0,1},{1,0},{16,17},{17,16},{2,3},{3,2},{18,19},{19,18},{4,5},{5,4... | collective-permute-start | bytes 3145736 | tf_op jit(solution)/shard_map/ppermute | solution.py:69
  186.4 47.4 %collective-permute-start.12 = (bf16[2,2,128,1024]{3,2,1,0:T(8,128)(2,1)S(1)}, bf16[2,2,128,1024]{3,2,1,0:T(8,128)(2,1)}, u32[]{:S(2)}, u32[]{:S(2)}) collective-permute-start(bf16[2,2,128,1024]{3,2,1,0:T(8,128)(2,1)S(1)} %get-tuple-element.116.refs_3_), channel_id=1, source_target_pairs={{0,16},{1,17},{16,0},{17,1},{2,18},{3,19},{18,2},{19,3},{4,20},{5,... | collective-permute-start | bytes 3145736 | tf_op jit(solution)/shard_map/ppermute | solution.py:69
  187.7 47.8 %collective-permute-start.13 = (bf16[2,2,128,1024]{3,2,1,0:T(8,128)(2,1)S(1)}, bf16[2,2,128,1024]{3,2,1,0:T(8,128)(2,1)}, u32[]{:S(2)}, u32[]{:S(2)}) collective-permute-start(bf16[2,2,128,1024]{3,2,1,0:T(8,128)(2,1)S(1)} %get-tuple-element.115.refs_4_), channel_id=1, source_target_pairs={{0,17},{1,16},{16,1},{17,0},{2,19},{3,18},{18,3},{19,2},{4,21},{5,... | collective-permute-start | bytes 3145736 | tf_op jit(solution)/shard_map/ppermute | solution.py:69
  252.0 12.2 %collective-permute-start.14 = (bf16[2,256,5120]{2,1,0:T(8,128)(2,1)}, bf16[2,256,5120]{2,1,0:T(8,128)(2,1)}, u32[]{:S(2)}, u32[]{:S(2)}) collective-permute-start(bf16[2,256,5120]{2,1,0:T(8,128)(2,1)} %get-tuple-element.71), channel_id=1, source_target_pairs={{0,8},{8,0},{1,9},{9,1},{2,10},{10,2},{3,11},{11,3},{4,12},{12,4},... | collective-permute-start | bytes 15728648 | tf_op jit(solution)/shard_map/ppermute | solution.py:69
  252.1 159.4 %reduce-scatter.8.cloned.1.call-start = ((), (), s32[]{:S(2)}) async-start(), calls=%async_computation.7 | async-start | bytes 1638400 | tf_op jit(solution)/shard_map/reduce_scatter | solution.py:219
  270.4 73.8 %collective-permute-start.16 = (bf16[2,2,32,5120]{3,2,1,0:T(8,128)(2,1)}, bf16[2,2,32,5120]{3,2,1,0:T(8,128)(2,1)S(1)}, u32[]{:S(2)}, u32[]{:S(2)}) collective-permute-start(bf16[2,2,32,5120]{3,2,1,0:T(8,128)(2,1)} %get-tuple-element.114.refs_4_), channel_id=1, source_target_pairs={{0,1},{1,0},{16,17},{17,16},{2,3},{3,2},{18,19},{19,18},{4,5},{5,4... | collective-permute-start | bytes 3932168 | tf_op jit(solution)/shard_map/ppermute | solution.py:69
  270.9 73.3 %collective-permute-start.17 = (bf16[2,2,32,5120]{3,2,1,0:T(8,128)(2,1)}, bf16[2,2,32,5120]{3,2,1,0:T(8,128)(2,1)S(1)}, u32[]{:S(2)}, u32[]{:S(2)}) collective-permute-start(bf16[2,2,32,5120]{3,2,1,0:T(8,128)(2,1)} %get-tuple-element.113.refs_5_), channel_id=1, source_target_pairs={{0,16},{1,17},{16,0},{17,1},{2,18},{3,19},{18,2},{19,3},{4,20},{5,... | collective-permute-start | bytes 3932168 | tf_op jit(solution)/shard_map/ppermute | solution.py:69
  271.5 72.7 %collective-permute-start.18 = (bf16[2,2,32,5120]{3,2,1,0:T(8,128)(2,1)}, bf16[2,2,32,5120]{3,2,1,0:T(8,128)(2,1)}, u32[]{:S(2)}, u32[]{:S(2)}) collective-permute-start(bf16[2,2,32,5120]{3,2,1,0:T(8,128)(2,1)} %get-tuple-element.112.refs_6_), channel_id=1, source_target_pairs={{0,17},{1,16},{16,1},{17,0},{2,19},{3,18},{18,3},{19,2},{4,21},{5,... | collective-permute-start | bytes 3932168 | tf_op jit(solution)/shard_map/ppermute | solution.py:69
  344.1 6.1 %collective-permute-start.15 = (bf16[3,512,1024]{2,1,0:T(8,128)(2,1)}, bf16[3,512,1024]{2,1,0:T(8,128)(2,1)}, u32[]{:S(2)}, u32[]{:S(2)}) collective-permute-start(bf16[3,512,1024]{2,1,0:T(8,128)(2,1)} %get-tuple-element.73), channel_id=1, source_target_pairs={{0,8},{8,0},{1,9},{9,1},{2,10},{10,2},{3,11},{11,3},{4,12},{12,4},... | collective-permute-start | bytes 9437192 | tf_op jit(solution)/shard_map/ppermute | solution.py:69
  349.4 67.8 %reduce-scatter.6.cloned.1.call-start = ((), (), s32[]{:S(2)}) async-start(), calls=%async_computation.6 | async-start | bytes 983040 | tf_op jit(solution)/shard_map/reduce_scatter | solution.py:219
  353.7 39.4 %collective-permute-start.25 = (bf16[3,2,2,32,1024]{4,3,2,1,0:T(8,128)(2,1)S(1)}, bf16[3,2,2,32,1024]{4,3,2,1,0:T(8,128)(2,1)S(1)}, u32[]{:S(2)}, u32[]{:S(2)}) collective-permute-start(bf16[3,2,2,32,1024]{4,3,2,1,0:T(8,128)(2,1)S(1)} %get-tuple-element.120.refs_8_), channel_id=1, source_target_pairs={{0,1},{1,0},{16,17},{17,16},{2,3},{3,2},{18,19},{19,18},{4,5},{5,4... | collective-permute-start | bytes 2359304 | tf_op jit(solution)/shard_map/ppermute | solution.py:69
  355.3 37.9 %collective-permute-start.26 = (bf16[3,2,2,32,1024]{4,3,2,1,0:T(8,128)(2,1)S(1)}, bf16[3,2,2,32,1024]{4,3,2,1,0:T(8,128)(2,1)}, u32[]{:S(2)}, u32[]{:S(2)}) collective-permute-start(bf16[3,2,2,32,1024]{4,3,2,1,0:T(8,128)(2,1)S(1)} %get-tuple-element.119.refs_9_), channel_id=1, source_target_pairs={{0,16},{1,17},{16,0},{17,1},{2,18},{3,19},{18,2},{19,3},{4,20},{5,... | collective-permute-start | bytes 2359304 | tf_op jit(solution)/shard_map/ppermute | solution.py:69
  356.7 36.4 %collective-permute-start.27 = (bf16[3,2,2,32,1024]{4,3,2,1,0:T(8,128)(2,1)S(1)}, bf16[3,2,2,32,1024]{4,3,2,1,0:T(8,128)(2,1)}, u32[]{:S(2)}, u32[]{:S(2)}) collective-permute-start(bf16[3,2,2,32,1024]{4,3,2,1,0:T(8,128)(2,1)S(1)} %get-tuple-element.118.refs_10_), channel_id=1, source_target_pairs={{0,17},{1,16},{16,1},{17,0},{2,19},{3,18},{18,3},{19,2},{4,21},{5,... | collective-permute-start | bytes 2359304 | tf_op jit(solution)/shard_map/ppermute | solution.py:69
  374.0 16.0 %collective-permute-start.19 = (f32[2,2,2,2,384]{4,3,2,1,0:T(2,128)S(1)}, f32[2,2,2,2,384]{4,3,2,1,0:T(2,128)S(1)}, u32[]{:S(2)}, u32[]{:S(2)}) collective-permute-start(f32[2,2,2,2,384]{4,3,2,1,0:T(2,128)S(1)} %dynamic-slice_bitcast_fusion), channel_id=1, source_target_pairs={{0,8},{8,0},{1,9},{9,1},{2,10},{10,2},{3,11},{11,3},{4,12},{12,4},... | collective-permute-start | bytes 73736 | tf_op jit(solution)/shard_map/ppermute | solution.py:69
  390.1 7.3 %collective-permute-start.20 = (f32[2,2,384]{2,1,0:T(2,128)S(1)}, f32[2,2,384]{2,1,0:T(2,128)S(1)}, u32[]{:S(2)}, u32[]{:S(2)}) collective-permute-start(f32[2,2,384]{2,1,0:T(2,128)S(1)} %bitcast_add_fusion.5), channel_id=1, source_target_pairs={{0,1},{1,0},{16,17},{17,16},{2,3},{3,2},{18,19},{19,18},{4,5},{5,4... | collective-permute-start | bytes 18440 | tf_op jit(solution)/shard_map/ppermute | solution.py:69
  391.6 5.8 %collective-permute-start.21 = (f32[2,2,384]{2,1,0:T(2,128)S(1)}, f32[2,2,384]{2,1,0:T(2,128)S(1)}, u32[]{:S(2)}, u32[]{:S(2)}) collective-permute-start(f32[2,2,384]{2,1,0:T(2,128)S(1)} %bitcast_add_fusion.4), channel_id=1, source_target_pairs={{0,16},{1,17},{16,0},{17,1},{2,18},{3,19},{18,2},{19,3},{4,20},{5,... | collective-permute-start | bytes 18440 | tf_op jit(solution)/shard_map/ppermute | solution.py:69
  396.8 4.6 %collective-permute-start.22 = (f32[2,2,384]{2,1,0:T(2,128)S(1)}, f32[2,2,384]{2,1,0:T(2,128)S(1)}, u32[]{:S(2)}, u32[]{:S(2)}) collective-permute-start(f32[2,2,384]{2,1,0:T(2,128)S(1)} %bitcast_add_fusion.3), channel_id=1, source_target_pairs={{0,17},{1,16},{16,1},{17,0},{2,19},{3,18},{18,3},{19,2},{4,21},{5,... | collective-permute-start | bytes 18440 | tf_op jit(solution)/shard_map/ppermute | solution.py:69
  401.4 3.7 collective-permute-start.23
  405.1 4.6 %collective-permute-start.24 = (f32[384]{0:T(512)S(1)}, f32[384]{0:T(512)S(1)}, u32[]{:S(2)}, u32[]{:S(2)}) collective-permute-start(f32[384]{0:T(512)S(1)} %add_add_fusion), channel_id=1, source_target_pairs={{0,4},{4,0},{1,5},{5,1},{2,6},{6,2},{3,7},{7,3},{8,12},{12,8},{9,1... | collective-permute-start | bytes 4616 | tf_op jit(solution)/shard_map/ppermute | solution.py:69
  (23 other events, 367.7 us)
Sparse Core Ops, SparseCore 0:
  11.5 110.7 all-gather.4
  125.3 76.7 all-gather.2
  252.2 39.5 reduce-scatter.3
  349.5 30.0 reduce-scatter.7
  396.9 20.3 reduce-scatter.5
where the time goes:
time: 434 us; the launch traced here: 426 us
  Pallas kernels  221 us (51%)
  waiting for transfers between devices  111 us (26%)
  other arithmetic  34.3 us (8%)
  starting transfers between devices  26.1 us (6%)
  local copies, waits for them, and re-layouts  19.5 us (4%)
  between operations  14.9 us (3%)
    ppermute x28, waiting for transfers between devices, send(): return lax.ppermute(value, names, pairs)  78.8 us
    pallas_call x1, Pallas kernels, attend_back(): pl.pallas_call(partial(attend_back_kernel, outer, len(after)), grid_spec=...  50.5 us
    pallas_call x4, Pallas kernels, half_grad(): pl.pallas_call(body, grid_spec=pltpu.PrefetchScalarGridSpec(num_scalar_pr...  41.7 us
    pallas_call x1, Pallas kernels, attend(): pl.pallas_call(partial(attend_kernel, qkv_all.layout, (qkv_all.count, len...  38.3 us
    pallas_call x1, Pallas kernels, feed_down(): pl.pallas_call(partial(feed_down_kernel, (up_out.layout, down.layout), (u...  31.7 us
    pallas_call x1, Pallas kernels, feed_up(): pl.pallas_call(partial(feed_up_kernel, up_out.layout, (up_out.count, len(...  26.9 us
    ppermute x28, starting transfers between devices, send(): return lax.ppermute(value, names, pairs)  25.9 us
    reduce_scatter x3, waiting for transfers between devices, along_z(): own = lax.psum_scatter(rows, ('zh', 'zl'), scatter_dimension=0, tiled=True)  19.4 us
  transfers between devices with their start and end apart: 33, of which 17 were waited for; matrix products, arithmetic and copies ran while one was open for 11% of the time, Pallas kernels for 49%

commit v1 on v0

--- a/solution.py
+++ b/solution.py
@@ -181,43 +181,54 @@
 
 
 class Scatter:
-    plane = ("y", "x")
-
     def __init__(self, grid, coords, arrays, axes):
         self.grid, self.coords = grid, coords
         self.terms = [Term(array, axes) for array in arrays]
-        self.steps = grid.offsets(self.plane)
-
-    def sends(self, wire=jnp.bfloat16):
-        self.sent = []
+
+    def sends(self, names, wire=jnp.bfloat16):
+        self.names, self.steps, self.sent = names, self.grid.offsets(names), []
         for step in self.steps:
             target = {
                 name: lax.rem(self.coords[name] + step[name], self.grid.sizes[name])
-                for name in self.plane
+                for name in names
             }
             self.sent.append(add_up(term.at(target).value() for term in self.terms).astype(wire))
         return self.sent
 
     def move(self, token):
         arrived = [self.grid.send(value, step) for value, step in zip(self.sent, self.steps)]
-        arrived = hold((arrived, token))[0]
-        own = {name: self.coords[name] for name in self.plane}
+        arrived, token = hold((arrived, token))
+        own = {name: self.coords[name] for name in self.names}
         self.terms = [term.at(own) for term in self.terms]
-        axes = tuple(axis for axis in self.terms[0].axes if axis not in own)
+        axes = tuple(axis for axis in self.terms[0].axes if axis not in self.terms[0].places)
         self.terms += [Term(value, axes) for value in arrived]
-        return arrived
-
-    def blocks(self, wire=jnp.bfloat16):
+        return token
+
+    def total(self):
+        return add_up(term.value() for term in self.terms)
+
+    def rows_z(self, wire=jnp.bfloat16):
         axes = [axis for axis in self.terms[0].axes if axis not in self.terms[0].places]
         lead = [axes.index(name) for name in ("zh", "zl")]
         value = add_up(jnp.moveaxis(term.value(), lead, (0, 1)) for term in self.terms)
         self.left = value.astype(wire).reshape(-1, *value.shape[2:])
+        self.axes = tuple(axis for axis in axes if axis not in ("zh", "zl"))
         return self.left
 
-    def along_z(self):
+    def along_z(self, token=None):
         rows = self.left.reshape(-1, self.left.shape[-1])
         own = lax.psum_scatter(rows, ("zh", "zl"), scatter_dimension=0, tiled=True)
-        return own.astype(jnp.float32).reshape(self.left.shape[1:])
+        if token is not None:
+            own, token = hold((own, token))
+        self.terms = [Term(own.reshape(self.left.shape[1:]), self.axes)]
+        return token
+
+
+def joined_sides(first, second, token):
+    arrays, _ = hold(([first.terms[0].value(), second.terms[0].value()], token))
+    sizes, rows = arrays[0].shape[:2], arrays[1].shape[2]
+    arrays = [array.reshape(*sizes, rows, -1) for array in arrays]
+    return Scatter(first.grid, first.coords, [jnp.concatenate(arrays, -1)], first.axes)
 
 
 def scatter_small(grid, coords, array, rounds):
@@ -733,64 +744,75 @@
     )(down.places, *down.pieces, *after, inner, hidden, shift.reshape(1, -1))
 
 
-def grad_kernel(outer, ends, core, *refs):
-    lefts, refs = refs[: outer * len(ends)], refs[outer * len(ends) :]
-    rights, out, mark, turned = refs[: len(ends)], refs[-3], refs[-2], refs[-1]
+def grad_kernel(outer, sides, plan, *refs):
+    span = outer * sides
+    lefts, refs = refs[: span * len(plan)], refs[span * len(plan) :]
+    count = sum(len(cuts) for _, cuts in plan)
+    rights, refs = refs[: len(plan)], refs[-2 - sides * count :]
+    outs, mark, turned = refs[:-2], refs[-2], refs[-1]
     mark[...] = jnp.zeros_like(mark)
     chunk_at = pl.program_id(1)
-    begin = 0
-    for pair, end in enumerate(ends):
+    begin, first_out = 0, 0
+    for pair, (chunks, cuts) in enumerate(plan):
 
         @pl.when(chunk_at == begin)
         def _(pair=pair):
-            for y in range(outer):
-                left = lefts[pair * outer + y][...]
-                turned[y * left.shape[1] : (y + 1) * left.shape[1], :] = left.T
-
-        @pl.when((chunk_at >= begin) & (chunk_at < end))
-        def _(pair=pair):
-            cots = rights[pair][...].reshape(rights[pair].shape[-2:])
-            out[...] = dot(turned[...], cots).astype(out.dtype).reshape(out.shape)
-
-        begin = end
-
-
-def half_grad(core, outer, pairs, after=(), block=256, chunk=1024):
+            for at in range(span):
+                left = lefts[pair * span + at][...]
+                turned[at * left.shape[1] : (at + 1) * left.shape[1], :] = left.T
+
+        @pl.when((chunk_at >= begin) & (chunk_at < begin + chunks))
+        def _(pair=pair, cuts=cuts, first_out=first_out):
+            cots = rights[pair][...]
+            rows = turned.shape[0] // sides
+            for side in range(sides):
+                grads = dot(turned[side * rows : (side + 1) * rows, :], cots).astype(jnp.bfloat16)
+                column = 0
+                for number, _ in enumerate(cuts):
+                    out = outs[side * count + first_out + number]
+                    wide = out.shape[2]
+                    out[...] = grads[:, column : column + wide].reshape(out.shape)
+                    column += wide
+
+        begin += chunks
+        first_out += len(cuts)
+
+
+def core_grads(cores, outer, pairs, after=(), block=256, chunk=1024):
     rows, width = pairs[0][0].shape
+    sides = len(cores)
     per_outer = width // (2 * outer)
     block = min(block, per_outer)
     steps = per_outer // block
-    ends, lefts, left_specs, right_specs, begin = [], [], [], [], 0
-    for left, right, first, span in pairs:
-        count, depth = span // chunk, right.shape[-1] // chunk
-        for y in range(outer):
-            lefts.append(left)
-            left_specs.append(
-                pl.BlockSpec(
-                    (rows, block), lambda m, n, c, y=y: (0, (y * 2 + c[0]) * steps + m)
+    low, struct = jnp.bfloat16, jax.ShapeDtypeStruct
+    plan, lefts, left_specs, right_specs, out_specs, outs, begin = [], [], [], [], [], [], 0
+    for left, right, cuts in pairs:
+        count = sum(cuts) // chunk
+        for side in range(sides):
+            for y in range(outer):
+                lefts.append(left)
+                left_specs.append(
+                    pl.BlockSpec(
+                        (rows, block),
+                        lambda m, n, c, y=y, side=side: (0, (y * 2 + c[side]) * steps + m),
+                    )
                 )
+
+        def at(n, begin=begin, count=count):
+            return jnp.clip(n - begin, 0, count - 1)
+
+        right_specs.append(pl.BlockSpec((rows, chunk), lambda m, n, c, at=at: (0, at(n))))
+        for cut in cuts:
+            out_specs.append(
+                pl.BlockSpec((outer, block, min(cut, chunk)), lambda m, n, c, at=at: (0, m, at(n)))
             )
-
-        def pick(n, begin=begin, count=count, first=first):
-            return first // chunk + jnp.clip(n - begin, 0, count - 1)
-
-        if right.ndim == 3:
-            right_specs.append(
-                pl.BlockSpec(
-                    (1, rows, chunk),
-                    lambda m, n, c, pick=pick, depth=depth: (pick(n) // depth, 0, pick(n) % depth),
-                )
-            )
-        else:
-            right_specs.append(
-                pl.BlockSpec((rows, chunk), lambda m, n, c, pick=pick: (0, pick(n)))
-            )
+            outs.append(struct((outer, per_outer, cut), low))
+        plan.append((count, cuts))
         begin += count
-        ends.append(begin)
     total = begin * chunk
 
-    def body(core, *refs):
-        grad_kernel(outer, ends, core, *refs[: -3 - len(after)], *refs[-3:])
+    def body(_, *refs):
+        grad_kernel(outer, sides, plan, *refs)
 
     return pl.pallas_call(
         body,
@@ -798,20 +820,17 @@
             num_scalar_prefetch=1,
             grid=(steps, begin),
             in_specs=left_specs + right_specs + [ANY] * len(after),
-            out_specs=[
-                pl.BlockSpec((outer, block, chunk), lambda m, n, c: (0, m, n)),
-                pl.BlockSpec((8, LANES), lambda m, n, c: (0, 0)),
-            ],
-            scratch_shapes=[pltpu.VMEM((outer * block, rows), jnp.bfloat16)],
+            out_specs=out_specs * sides + [pl.BlockSpec((8, LANES), lambda m, n, c: (0, 0))],
+            scratch_shapes=[pltpu.VMEM((sides * outer * block, rows), low)],
         ),
-        out_shape=[
-            jax.ShapeDtypeStruct((outer, per_outer, total), jnp.bfloat16),
-            jax.ShapeDtypeStruct((8, LANES), jnp.float32),
-        ],
+        out_shape=outs * sides + [struct((8, LANES), jnp.float32)],
         compiler_params=params(),
-        cost_estimate=cost(rows * width * total, rows * (width + 2 * total) + width * total),
-        name="half_grad",
-    )(core.reshape(1), *lefts, *[pair[1] for pair in pairs], *after)
+        cost_estimate=cost(
+            sides * rows * width * total,
+            rows * (sides * width + 2 * total) + sides * width * total,
+        ),
+        name="core_grads",
+    )(jnp.stack(cores), *lefts, *[pair[1] for pair in pairs], *after)
 
 
 def cells_kernel(layout, counts, places, *refs):
@@ -951,26 +970,33 @@
     def shared(product):
         return product.reshape(block_sizes + [-1, product.shape[-1]])
 
-    def start(pairs, after=()):
-        sent, mark = half_grad(other, outer, pairs, after)
-        return mark, grid.send(sent, {"core": 1})
-
-    def under_way(kept, arrived):
+    def under_way(kept, sent):
+        arrived = grid.send(sent, {"core": 1})
         return Scatter(grid, coords, [shared(kept), shared(arrived)], block_axes)
 
-    down_pairs = [(hidden, out_grad, 0, width)]
-    down_mark, down_core = start(down_pairs)
-    down_kept, _ = half_grad(mine, outer, down_pairs, [down_mark])
-    down_sum = under_way(down_kept, down_core)
+    plane, line_z = ("y", "x"), ("zh", "zl")
+    quarter = width // 4
+    down_pairs = [(hidden, out_grad, (width - quarter, quarter))]
+    sent, sent_side, mark = core_grads([other], outer, down_pairs)
+    kept, kept_side, _ = core_grads([mine], outer, down_pairs, [mark])
+    down_sum, down_side = under_way(kept, sent), under_way(kept_side, sent_side)
     d_up, d_inner, e_rows, d_mixed, sums, up_sums = feed_down(
-        up_out, down_all, inner, slopes, out_grad, rows_two, down_sum.sends()
-    )
-    up_pairs = [(normed_two, d_up, 0, wide), (mixed, e_rows, 0, width)]
-    down_sum.move(sums)
-    up_mark, up_core = start(up_pairs, [down_sum.blocks()])
-    down_total = down_sum.along_z()
-    up_kept, _ = half_grad(mine, outer, up_pairs, [up_mark])
-    up_sum = under_way(up_kept, up_core)
+        up_out,
+        down_all,
+        inner,
+        slopes,
+        out_grad,
+        rows_two,
+        down_sum.sends(plane) + [down_side.rows_z()],
+    )
+    sums = down_sum.move(down_side.along_z(sums))
+    up_pairs = [(normed_two, d_up, (wide,)), (mixed, e_rows, (width,))]
+    sent, sent_side, kept, kept_side, _ = core_grads(
+        [other, mine], outer, up_pairs, down_sum.sends(line_z)
+    )
+    sent, sent_side = down_sum.move((sent, sent_side))
+    down_main = down_sum.total()
+    up_sum, out_sum = under_way(kept, sent), under_way(kept_side, sent_side)
     d_qkv, qv_sums, qkv_sent, qkv_kept = attend_back(
         mine,
         outer,
@@ -980,8 +1006,10 @@
         log_sums,
         d_mixed,
         normed,
-        up_sum.sends() + [down_total],
-    )
+        up_sum.sends(plane) + [down_main, out_sum.rows_z(), down_side.terms[0].array],
+    )
+    qv_sums, qkv_sent = up_sum.move((qv_sums, qkv_sent))
+    qkv_sent = out_sum.along_z(qkv_sent)
     qkv_core = grid.send(qkv_sent, {"core": 1})
     qkv_sum = Scatter(
         grid,
@@ -989,18 +1017,14 @@
         [term.reshape([3] + block_sizes + [-1, width]) for term in (qkv_kept, qkv_core)],
         ("part",) + block_axes,
     )
-    qkv_sends = qkv_sum.sends()
-    up_moved = up_sum.move((qv_sums, qkv_sends[-1][:, 0, 0, :8, :LANES]))
     cells_grad, one_sums = cells_back(
-        qkv_all, d_qkv, cells, d_inner, gain_one, qkv_sends + up_moved
-    )
-    up_blocks = up_sum.blocks()
-    up_total = up_sum.along_z()
-    out_cells = output(down_all, inner, hidden, b_down, [one_sums, up_blocks])
-    ahead = qkv_sum.move(out_cells)
-    qkv_sum.blocks()
-    qkv_total = qkv_sum.along_z()
-
+        qkv_all,
+        d_qkv,
+        cells,
+        d_inner,
+        gain_one,
+        qkv_sum.sends(plane) + [up_sum.rows_z()],
+    )
     vector_grads = (
         one_sums[0],
         one_sums[1],
@@ -1013,9 +1037,33 @@
     )
     sizes = [grid.sizes[name] for name in AXES]
     stacked = jnp.concatenate([grad.reshape(*sizes, -1) for grad in vector_grads], -1)
-    summed = scatter_small(
-        grid, coords, stacked, (("core",), ("y", "x"), ("zl",), ("zh",))
-    )
+    vector_sum = Scatter(grid, coords, [stacked], AXES)
+    side_sum = joined_sides(down_side, out_sum, one_sums)
+    out_cells = output(
+        down_all,
+        inner,
+        hidden,
+        b_down,
+        vector_sum.sends(("core",), jnp.float32) + side_sum.sends(("y",)),
+    )
+    out_cells = qkv_sum.move(out_cells)
+    qkv_sum.left = up_sum.along_z(side_sum.move(vector_sum.move(qkv_sum.rows_z())))
+    up_total = up_sum.total()
+    qkv_sum.along_z()
+    vector_sum.sends(plane, jnp.float32)
+    vector_sum.move(())
+    vector_sum.sends(line_z, jnp.float32)
+    vector_sum.move(())
+    side_sum.sends(("x",))
+    side_sum.move(())
+    summed = vector_sum.total()
+    qkv_total = qkv_sum.total()
+    side_total = side_sum.total()
+    rest = quarter * down_main.shape[0] // own_rows
+    down_total = jnp.concatenate(
+        [down_main, side_total[:, :rest].reshape(down_main.shape[0], quarter)], 1
+    )
+    out_total = side_total[:, rest:]
     parts, first = [], 0
     for vector in vectors:
         parts.append(summed[first : first + vector.shape[0]])
@@ -1027,11 +1075,11 @@
         parts[1],
         jnp.concatenate([qkv_total[part] for part in range(3)], 1),
         parts[2],
-        up_total[:, wide:],
+        out_total,
         parts[3],
         parts[4],
         parts[5],
-        up_total[:, :wide],
+        up_total,
         parts[6],
         down_total,
         parts[7],

time: 434 us -> 436 us (level)
  starting transfers between devices: 26.1 us -> 41.6 us
  waiting for transfers between devices: 111 us -> 97.3 us
    ppermute x28 -> x36, starting transfers between devices: 25.9 us -> 40.9 us  [send(): return lax.ppermute(value, names, pairs)]
    reduce_scatter x3 -> x4, waiting for transfers between devices: 19.4 us -> 9.35 us  [along_z(): own = lax.psum_scatter(rows, ('zh', 'zl'), scatter_dimension=0, tiled=True)]
    pallas_call x4 -> x3, Pallas kernels: 41.7 us -> 37.5 us  [core_grads(): pl.pallas_call(body, grid_spec=pltpu.PrefetchScalarGridSpec(num_scalar_pr...]
    convert_element_type x4 -> x5, other arithmetic: 14.2 us -> 11.5 us  [the longest x4 10.7 us: rows_z(): self.left = value.astype(wire).reshape(-1, *value.shape[2:])]
    ppermute x28 -> x36, waiting for transfers between devices: 78.8 us -> 77.3 us  [send(): return lax.ppermute(value, names, pairs)]
    convert_element_type x3 -> x5, other arithmetic: 14.3 us -> 14.1 us  [sends(): add_up((term.at(target).value() for term in self.terms)).astype(wire)]
  transfers between devices with their start and end apart: 33 -> 42, of which waited for: 17 -> 15; matrix products, arithmetic and copies ran while one was open for 11% -> 11% of each run, Pallas kernels for 49% -> 51%
where the time goes in v1:
time: 436 us; the launch traced here: 428 us
  Pallas kernels  217 us (50%)
  waiting for transfers between devices  97.3 us (22%)
  starting transfers between devices  41.6 us (10%)
  other arithmetic  35.1 us (8%)
  local copies, waits for them, and re-layouts  22.1 us (5%)
  between operations  15.5 us (4%)
    ppermute x36, waiting for transfers between devices, send(): return lax.ppermute(value, names, pairs)  77.3 us
    pallas_call x1, Pallas kernels, attend_back(): pl.pallas_call(partial(attend_back_kernel, outer, len(after)), grid_spec=...  50.5 us
    ppermute x36, starting transfers between devices, send(): return lax.ppermute(value, names, pairs)  40.9 us
    pallas_call x1, Pallas kernels, attend(): pl.pallas_call(partial(attend_kernel, qkv_all.layout, (qkv_all.count, len...  38.3 us
    pallas_call x3, Pallas kernels, core_grads(): pl.pallas_call(body, grid_spec=pltpu.PrefetchScalarGridSpec(num_scalar_pr...  37.5 us
    pallas_call x1, Pallas kernels, feed_down(): pl.pallas_call(partial(feed_down_kernel, (up_out.layout, down.layout), (u...  32 us
    pallas_call x1, Pallas kernels, feed_up(): pl.pallas_call(partial(feed_up_kernel, up_out.layout, (up_out.count, len(...  26.9 us
    pallas_call x1, Pallas kernels, output(): pl.pallas_call(partial(output_kernel, down.layout, (down.count, len(after...  15.7 us
  transfers between devices with their start and end apart: 42, of which 15 were waited for; matrix products, arithmetic and copies ran while one was open for 11% of the time, Pallas kernels for 51%

profile of v1, /device:TPU:0, one launch (start us, length us, event | category | flops | bytes accessed | tf_op | source)
XLA Modules:
  0.0 428.3 jit_solution(400841126265600591)
XLA Ops:
  13.4 3.1 collective-permute-start
  16.5 2.6 collective-permute-start.1
  19.1 6.1 %collective-permute-done = bf16[1,32,3200]{2,1,0:T(8,128)(2,1)S(1)} collective-permute-done((bf16[1,32,3200]{2,1,0:T(8,128)(2,1)S(1)}, bf16[1,32,3200]{2,1,0:T(8,128)(2,1)S(1)}, u32[]{:S(2)}, u32[]{:S(2)}) %collective-permute-start) | collective-permute-done | bytes 204832 | tf_op jit(solution)/shard_map/ppermute | solution.py:69
  25.2 12.2 %collective-permute-done.1 = bf16[1,32,3200]{2,1,0:T(8,128)(2,1)S(1)} collective-permute-done((bf16[1,32,3200]{2,1,0:T(8,128)(2,1)S(1)}, bf16[1,32,3200]{2,1,0:T(8,128)(2,1)S(1)}, u32[]{:S(2)}, u32[]{:S(2)}) %collective-permute-start.1) | collective-permute-done | bytes 204832 | tf_op jit(solution)/shard_map/ppermute | solution.py:69
  41.0 25.3 %collective-permute-done.3.refs_1_ = bf16[4,32,3200]{2,1,0:T(8,128)(2,1)S(1)} collective-permute-done((bf16[4,32,3200]{2,1,0:T(8,128)(2,1)S(1)}, bf16[4,32,3200]{2,1,0:T(8,128)(2,1)S(1)}, u32[]{:S(2)}, u32[]{:S(2)}) %collective-permute-start.3) | collective-permute-done | bytes 819232 | tf_op jit(solution)/shard_map/ppermute | solution.py:69
  66.3 16.6 %collective-permute-done.5.refs_3_ = bf16[4,32,3200]{2,1,0:T(8,128)(2,1)S(1)} collective-permute-done((bf16[4,32,3200]{2,1,0:T(8,128)(2,1)S(1)}, bf16[4,32,3200]{2,1,0:T(8,128)(2,1)S(1)}, u32[]{:S(2)}, u32[]{:S(2)}) %collective-permute-start.5) | collective-permute-done | bytes 819232 | tf_op jit(solution)/shard_map/ppermute | solution.py:69
  96.7 38.3 %attend.1 = (bf16[1024,1024]{1,0:T(8,128)(2,1)}, bf16[3,1024,1024]{2,1,0:T(8,128)(2,1)}, bf16[1024,1024]{1,0:T(8,128)(2,1)}, f32[8,2,1024]{2,1,0:T(2,128)}) custom-call(s32[32]{0:T(128)} %stack.240.places, bf16[4,32,3200]{2,1,0:T(8,128)(2,1)} %copy-done, bf16[4,32,3200]{2,1,0:T(8,128)(2,1)} %copy-done.5, bf16[4,32,3200]{2,1,0:T(8,128)(2,1)} %copy-done.6, ...), custom_call_target="tpu_custom_call" | custom-call | flops 1875000064 | bytes 1179648 | tf_op jit(solution)/shard_map/attend/pallas_call | solution.py:357
  135.7 26.9 %feed_up.1 = (f32[1024,1024]{1,0:T(8,128)}, bf16[1024,1024]{1,0:T(8,128)(2,1)}, bf16[1024,4096]{1,0:T(8,128)(2,1)}, bf16[1024,4096]{1,0:T(8,128)(2,1)}) custom-call(s32[1]{0:T(128)} %constant.81.clone.1.places.places_up.places_down, bf16[1,1024,5120]{2,1,0:T(8,128)(2,1)} %bitcast.286, ...), custom_call_target="tpu_custom_call" | custom-call | flops 671088640 | bytes 2097152 | tf_op jit(solution)/shard_map/feed_up/pallas_call | solution.py:573
  162.7 8.5 %core_grads.3 = (bf16[2,1024,768]{2,1,0:T(8,128)(2,1)}, bf16[2,1024,256]{2,1,0:T(8,128)(2,1)}, f32[8,128]{1,0:T(8,128)}) custom-call(s32[1]{0:T(128)} %bitcast.81._, bf16[1024,4096]{1,0:T(8,128)(2,1)} %get-tuple-element.84.refs_0_.refs_1_.refs_4_, bf16[1024,4096]{1,0:T(8,128)(2,1)} %get-tuple-element.84.refs_0_.refs_1_.refs_4_, bf16[1024,1024]{1,0:T(8,128)(2,1)} %refs_8_.3), custom_call_target="tpu_custom_call" | custom-call | flops 268435456 | bytes 655360 | tf_op jit(solution)/shard_map/core_grads/pallas_call | solution.py:817
  171.7 9.3 %core_grads.4 = (bf16[2,1024,768]{2,1,0:T(8,128)(2,1)}, bf16[2,1024,256]{2,1,0:T(8,128)(2,1)}, f32[8,128]{1,0:T(8,128)}) custom-call(s32[1]{0:T(128)} %bitcast._.core, bf16[1024,4096]{1,0:T(8,128)(2,1)} %get-tuple-element.84.refs_0_.refs_1_.refs_4_, bf16[1024,4096]{1,0:T(8,128)(2,1)} %get-tuple-element.84.refs_0_.refs_1_.refs_4_, ...), custom_call_target="tpu_custom_call" | custom-call | flops 268435456 | bytes 655360 | tf_op jit(solution)/shard_map/core_grads/pallas_call | solution.py:817
  181.0 1.8 add_convert_fusion.4
  184.0 4.5 %fusion.11 = (bf16[2,2,128,768]{3,2,1,0:T(8,128)(2,1)}, bf16[2,2,128,768]{3,2,1,0:T(8,128)(2,1)}, bf16[2,2,128,768]{3,2,1,0:T(8,128)(2,1)}) fusion(bf16[2,2,2,2,128,768]{5,4,3,2,1,0:T(8,128)(2,1)S(1)} %bitcast.302, s32[]{:T(128)S(6)} %select_n.40, s32[]{:T(128)S(6)} %select_n.39, bf16[2,2,2,2,128,768]{5,4,3,2,1,0:T(8,128)(2,1)} %bitcast.305, ...), kind=kLoop, calls=%fused_computation.26 | loop fusion | flops 4718592 | bytes 7077904 | tf_op jit(solution)/shard_map/convert_element_type | solution.py:195
  192.0 10.6 %all-gather.5.cloned.1.call-done = bf16[4096,1024]{1,0:T(8,128)(2,1)} async-done(((bf16[128,1024]{1,0:T(8,128)(2,1)}), bf16[4096,1024]{1,0:T(8,128)(2,1)}) %all-gather.5.cloned.1.call-update) | async-done | bytes 8388624 | tf_op jit(solution)/shard_map/all_gather | solution.py:946
  202.5 32.0 %feed_down.1 = (bf16[1024,4096]{1,0:T(8,128)(2,1)}, f32[1024,1024]{1,0:T(8,128)}, bf16[1024,1024]{1,0:T(8,128)(2,1)}, bf16[1024,1024]{1,0:T(8,128)(2,1)}, f32[4,1024]{1,0:T(4,128)}, /*index=5*/f32[1,4096]{1,0:T(1,128)}) custom-call(s32[1]{0:T(128)} %constant.81.clone.1.places.places_up.places_down, s32[1]{0:T(128)} %constant.81.clone.1.places.places_up.places_down, ...), custom_call_target="tpu_custom_call" | custom-call | flops 1207959552 | bytes 3145728 | tf_op jit(solution)/shard_map/feed_down/pallas_call | solution.py:657
  234.7 2.1 fusion.19
  236.8 6.6 %collective-permute-start.15 = (bf16[128,768]{1,0:T(8,128)(2,1)S(1)}, bf16[128,768]{1,0:T(8,128)(2,1)S(1)}, u32[]{:S(2)}, u32[]{:S(2)}) collective-permute-start(bf16[128,768]{1,0:T(8,128)(2,1)S(1)} %get-tuple-element.182.refs_10_), channel_id=1, source_target_pairs={{0,2},{2,0},{4,6},{6,4},{1,3},{3,1},{5,7},{7,5},{8,10},{10,8},{12,... | collective-permute-start | bytes 589832 | tf_op jit(solution)/shard_map/ppermute | solution.py:69
  243.4 2.1 collective-permute-start.16
  247.5 19.6 %core_grads.5 = (bf16[2,256,4096]{2,1,0:T(8,128)(2,1)}, bf16[2,256,1024]{2,1,0:T(8,128)(2,1)}, bf16[2,256,4096]{2,1,0:T(8,128)(2,1)}, bf16[2,256,1024]{2,1,0:T(8,128)(2,1)}, f32[8,128]{1,0:T(8,128)}) custom-call(s32[2]{0:T(128)} %pad_add_fusion._, bf16[1024,1024]{1,0:T(8,128)(2,1)} %get-tuple-element.94.refs_0_.refs_1_.refs_2_.refs_3_, ...), custom_call_target="tpu_custom_call" | custom-call | flops 671088640 | bytes 1441792 | tf_op jit(solution)/shard_map/core_grads/pallas_call | solution.py:817
  267.7 8.0 %collective-permute-done.19 = bf16[2,256,1024]{2,1,0:T(8,128)(2,1)S(1)} collective-permute-done((bf16[2,256,1024]{2,1,0:T(8,128)(2,1)}, bf16[2,256,1024]{2,1,0:T(8,128)(2,1)S(1)}, u32[]{:S(2)}, u32[]{:S(2)}) %collective-permute-start.19) | collective-permute-done | bytes 1048608 | tf_op jit(solution)/shard_map/ppermute | solution.py:69
  278.7 4.0 fusion.8
  287.4 2.3 fusion.18.refs_7_
  289.7 50.5 %attend_back.1 = (bf16[3,1024,1024]{2,1,0:T(8,128)(2,1)}, f32[2,1024]{1,0:T(2,128)}, bf16[3,512,1024]{2,1,0:T(8,128)(2,1)}, bf16[3,512,1024]{2,1,0:T(8,128)(2,1)}) custom-call(s32[1]{0:T(128)} %bitcast._.core, s32[1024,1]{1,0:T(8,128)} %copy.50.refs_12_.ids_col, s32[1,1024]{1,0:T(1,128)} %ids_row.1, s32[1024,1]{1,0:T(8,128)} %copy.51.live_col, ...), custom_call_target="tpu_custom_call" | custom-call | flops 2750000128 | bytes 1835008 | tf_op jit(solution)/shard_map/attend_back/pallas_call | solution.py:491
  341.5 4.3 %fusion.2 = bf16[2,2,32,4096]{3,2,1,0:T(8,128)(2,1)} fusion(bf16[2,2,32,4096]{3,2,1,0:T(8,128)(2,1)} %collective-permute-done.22, bf16[2,2,32,4096]{3,2,1,0:T(8,128)(2,1)} %collective-permute-done.21, bf16[2,2,32,4096]{3,2,1,0:T(8,128)(2,1)} %collective-permute-done.20, bf16[2,2,2,2,32,4096]{5,4,3,2,1,0:T(8,128)(2,1)} %bitcast.104, s32[]{:T(128)S(6)} %select_n.42, ...), kind=kLoop, calls=%fused_computation.4 | loop fusion | flops 5242880 | bytes 6291464 | tf_op jit(solution)/shard_map/convert_element_type | solution.py:214
  347.9 3.5 fusion.14
  355.0 15.6 %cells_back.1 = (bf16[1024,1024]{1,0:T(8,128)(2,1)}, f32[2,1024]{1,0:T(2,128)}) custom-call(s32[32]{0:T(128)} %stack.240.places, bf16[4,32,3200]{2,1,0:T(8,128)(2,1)} %copy-done, bf16[4,32,3200]{2,1,0:T(8,128)(2,1)} %copy-done.5, bf16[4,32,3200]{2,1,0:T(8,128)(2,1)} %copy-done.6, bf16[4,32,3200]{2,1,0:T(8,128)(2,1)} %copy-done.7, ...), custom_call_target="tpu_custom_call" | custom-call | flops 402653184 | bytes 1310720 | tf_op jit(solution)/shard_map/cells_back/pallas_call | solution.py:867
  373.0 15.7 %output.1 = bf16[1024,1024]{1,0:T(8,128)(2,1)} custom-call(s32[1]{0:T(128)} %constant.81.clone.1.places.places_up.places_down, bf16[1,4096,1024]{2,1,0:T(8,128)(2,1)} %bitcast.289, f32[2,2,2,2,384]{4,3,2,1,0:T(2,128)} %copy-done.27, bf16[2,32,2048]{2,1,0:T(8,128)(2,1)} %copy-done.17, f32[1024,1024]{1,0:T(8,128)} %get-tuple-element.90.refs_6_.refs_3_, ...), custom_call_target="tpu_custom_call" | custom-call | flops 536870912 | bytes 1572864 | tf_op jit(solution)/shard_map/output/pallas_call | solution.py:728
  388.8 2.9 fusion.5
  393.0 2.0 collective-permute-start.29
  396.7 2.0 collective-permute-done.28
  398.8 2.5 collective-permute-start.33
  401.4 1.9 collective-permute-start.31
  410.0 9.3 %reduce-scatter.11.cloned.1.call-done = bf16[96,1024]{1,0:T(8,128)(2,1)} async-done(((bf16[384,1024]{1,0:T(8,128)(2,1)}), bf16[96,1024]{1,0:T(8,128)(2,1)}) %reduce-scatter.11.cloned.1.call-update) | async-done | bytes 196624 | tf_op jit(solution)/shard_map/reduce_scatter | solution.py:220
  (225 shorter events, 60.0 us)
Async XLA Ops:
  7.2 128.5 %all-gather.3.cloned.1.call-start = ((), (), s32[]{:S(2)}) async-start(), calls=%async_computation.4 | async-start | bytes 10813440 | tf_op jit(solution)/shard_map/all_gather | solution.py:937
  9.0 193.5 %all-gather.5.cloned.1.call-start = ((), (), s32[]{:S(2)}) async-start(), calls=%async_computation.5 | async-start | bytes 8650752 | tf_op jit(solution)/shard_map/all_gather | solution.py:946
  13.4 11.8 %collective-permute-start = (bf16[1,32,3200]{2,1,0:T(8,128)(2,1)S(1)}, bf16[1,32,3200]{2,1,0:T(8,128)(2,1)S(1)}, u32[]{:S(2)}, u32[]{:S(2)}) collective-permute-start(bf16[1,32,3200]{2,1,0:T(8,128)(2,1)S(1)} %fusion.25), channel_id=1, source_target_pairs={{0,2},{2,0},{4,6},{6,4},{1,3},{3,1},{5,7},{7,5},{8,10},{10,8},{12,... | collective-permute-start | bytes 614408 | tf_op jit(solution)/shard_map/ppermute | solution.py:69
  16.5 20.9 %collective-permute-start.1 = (bf16[1,32,3200]{2,1,0:T(8,128)(2,1)S(1)}, bf16[1,32,3200]{2,1,0:T(8,128)(2,1)S(1)}, u32[]{:S(2)}, u32[]{:S(2)}) collective-permute-start(bf16[1,32,3200]{2,1,0:T(8,128)(2,1)S(1)} %fusion.25), channel_id=1, source_target_pairs={{0,4},{2,6},{4,0},{6,2},{1,5},{3,7},{5,1},{7,3},{8,12},{10,14},{12... | collective-permute-start | bytes 614408 | tf_op jit(solution)/shard_map/ppermute | solution.py:69
  19.0 18.3 %collective-permute-start.2 = (bf16[1,32,3200]{2,1,0:T(8,128)(2,1)S(1)}, bf16[1,32,3200]{2,1,0:T(8,128)(2,1)S(1)}, u32[]{:S(2)}, u32[]{:S(2)}) collective-permute-start(bf16[1,32,3200]{2,1,0:T(8,128)(2,1)S(1)} %fusion.25), channel_id=1, source_target_pairs={{0,6},{2,4},{4,2},{6,0},{1,7},{3,5},{5,3},{7,1},{8,14},{10,12},{12... | collective-permute-start | bytes 614408 | tf_op jit(solution)/shard_map/ppermute | solution.py:69
  37.5 28.8 %collective-permute-start.3 = (bf16[4,32,3200]{2,1,0:T(8,128)(2,1)S(1)}, bf16[4,32,3200]{2,1,0:T(8,128)(2,1)S(1)}, u32[]{:S(2)}, u32[]{:S(2)}) collective-permute-start(bf16[4,32,3200]{2,1,0:T(8,128)(2,1)S(1)} %pad_maximum_fusion.refs_0_), channel_id=1, source_target_pairs={{0,1},{1,0},{16,17},{17,16},{2,3},{3,2},{18,19},{19,18},{4,5},{5,4... | collective-permute-start | bytes 2457608 | tf_op jit(solution)/shard_map/ppermute | solution.py:69
  39.0 27.3 %collective-permute-start.4 = (bf16[4,32,3200]{2,1,0:T(8,128)(2,1)S(1)}, bf16[4,32,3200]{2,1,0:T(8,128)(2,1)S(1)}, u32[]{:S(2)}, u32[]{:S(2)}) collective-permute-start(bf16[4,32,3200]{2,1,0:T(8,128)(2,1)S(1)} %pad_maximum_fusion.refs_0_), channel_id=1, source_target_pairs={{0,16},{1,17},{16,0},{17,1},{2,18},{3,19},{18,2},{19,3},{4,20},{5,... | collective-permute-start | bytes 2457608 | tf_op jit(solution)/shard_map/ppermute | solution.py:69
  40.5 42.4 %collective-permute-start.5 = (bf16[4,32,3200]{2,1,0:T(8,128)(2,1)S(1)}, bf16[4,32,3200]{2,1,0:T(8,128)(2,1)S(1)}, u32[]{:S(2)}, u32[]{:S(2)}) collective-permute-start(bf16[4,32,3200]{2,1,0:T(8,128)(2,1)S(1)} %pad_maximum_fusion.refs_0_), channel_id=1, source_target_pairs={{0,17},{1,16},{16,1},{17,0},{2,19},{3,18},{18,3},{19,2},{4,21},{5,... | collective-permute-start | bytes 2457608 | tf_op jit(solution)/shard_map/ppermute | solution.py:69
  82.9 151.7 %reduce-scatter.5.cloned.1.call-start = ((), (), s32[]{:S(2)}) async-start(), calls=%async_computation.6 | async-start | bytes 1310720 | tf_op jit(solution)/shard_map/reduce_scatter | solution.py:220
  171.2 12.8 %collective-permute-start.10 = (bf16[2,1024,768]{2,1,0:T(8,128)(2,1)}, bf16[2,1024,768]{2,1,0:T(8,128)(2,1)S(1)}, u32[]{:S(2)}, u32[]{:S(2)}) collective-permute-start(bf16[2,1024,768]{2,1,0:T(8,128)(2,1)} %get-tuple-element.87), channel_id=1, source_target_pairs={{0,8},{8,0},{1,9},{9,1},{2,10},{10,2},{3,11},{11,3},{4,12},{12,4},... | collective-permute-start | bytes 9437192 | tf_op jit(solution)/shard_map/ppermute | solution.py:69
  171.3 9.7 %collective-permute-start.11 = (bf16[2,1024,256]{2,1,0:T(8,128)(2,1)}, bf16[2,1024,256]{2,1,0:T(8,128)(2,1)}, u32[]{:S(2)}, u32[]{:S(2)}) collective-permute-start(bf16[2,1024,256]{2,1,0:T(8,128)(2,1)} %get-tuple-element.89), channel_id=1, source_target_pairs={{0,8},{8,0},{1,9},{9,1},{2,10},{10,2},{3,11},{11,3},{4,12},{12,4},... | collective-permute-start | bytes 3145736 | tf_op jit(solution)/shard_map/ppermute | solution.py:69
  183.9 156.3 %reduce-scatter.7.cloned.1.call-start = ((), (), s32[]{:S(2)}) async-start(), calls=%async_computation.7 | async-start | bytes 1310720 | tf_op jit(solution)/shard_map/reduce_scatter | solution.py:220
  188.5 46.2 %collective-permute-start.12 = (bf16[2,2,128,768]{3,2,1,0:T(8,128)(2,1)}, bf16[2,2,128,768]{3,2,1,0:T(8,128)(2,1)}, u32[]{:S(2)}, u32[]{:S(2)}) collective-permute-start(bf16[2,2,128,768]{3,2,1,0:T(8,128)(2,1)} %get-tuple-element.191.refs_2_), channel_id=1, source_target_pairs={{0,1},{1,0},{16,17},{17,16},{2,3},{3,2},{18,19},{19,18},{4,5},{5,4... | collective-permute-start | bytes 2359304 | tf_op jit(solution)/shard_map/ppermute | solution.py:69
  189.6 45.0 %collective-permute-start.13 = (bf16[2,2,128,768]{3,2,1,0:T(8,128)(2,1)}, bf16[2,2,128,768]{3,2,1,0:T(8,128)(2,1)}, u32[]{:S(2)}, u32[]{:S(2)}) collective-permute-start(bf16[2,2,128,768]{3,2,1,0:T(8,128)(2,1)} %get-tuple-element.190.refs_3_), channel_id=1, source_target_pairs={{0,16},{1,17},{16,0},{17,1},{2,18},{3,19},{18,2},{19,3},{4,20},{5,... | collective-permute-start | bytes 2359304 | tf_op jit(solution)/shard_map/ppermute | solution.py:69
  191.0 43.6 %collective-permute-start.14 = (bf16[2,2,128,768]{3,2,1,0:T(8,128)(2,1)}, bf16[2,2,128,768]{3,2,1,0:T(8,128)(2,1)}, u32[]{:S(2)}, u32[]{:S(2)}) collective-permute-start(bf16[2,2,128,768]{3,2,1,0:T(8,128)(2,1)} %get-tuple-element.189.refs_4_), channel_id=1, source_target_pairs={{0,17},{1,16},{16,1},{17,0},{2,19},{3,18},{18,3},{19,2},{4,21},{5,... | collective-permute-start | bytes 2359304 | tf_op jit(solution)/shard_map/ppermute | solution.py:69
  236.8 30.3 %collective-permute-start.15 = (bf16[128,768]{1,0:T(8,128)(2,1)S(1)}, bf16[128,768]{1,0:T(8,128)(2,1)S(1)}, u32[]{:S(2)}, u32[]{:S(2)}) collective-permute-start(bf16[128,768]{1,0:T(8,128)(2,1)S(1)} %get-tuple-element.182.refs_10_), channel_id=1, source_target_pairs={{0,2},{2,0},{4,6},{6,4},{1,3},{3,1},{5,7},{7,5},{8,10},{10,8},{12,... | collective-permute-start | bytes 589832 | tf_op jit(solution)/shard_map/ppermute | solution.py:69
  243.4 23.7 %collective-permute-start.16 = (bf16[128,768]{1,0:T(8,128)(2,1)S(1)}, bf16[128,768]{1,0:T(8,128)(2,1)S(1)}, u32[]{:S(2)}, u32[]{:S(2)}) collective-permute-start(bf16[128,768]{1,0:T(8,128)(2,1)S(1)} %get-tuple-element.181.refs_11_), channel_id=1, source_target_pairs={{0,4},{2,6},{4,0},{6,2},{1,5},{3,7},{5,1},{7,3},{8,12},{10,14},{12... | collective-permute-start | bytes 589832 | tf_op jit(solution)/shard_map/ppermute | solution.py:69
  245.5 21.7 %collective-permute-start.17 = (bf16[128,768]{1,0:T(8,128)(2,1)S(1)}, bf16[128,768]{1,0:T(8,128)(2,1)S(1)}, u32[]{:S(2)}, u32[]{:S(2)}) collective-permute-start(bf16[128,768]{1,0:T(8,128)(2,1)S(1)} %get-tuple-element.180.refs_12_), channel_id=1, source_target_pairs={{0,6},{2,4},{4,2},{6,0},{1,7},{3,5},{5,3},{7,1},{8,14},{10,12},{12... | collective-permute-start | bytes 589832 | tf_op jit(solution)/shard_map/ppermute | solution.py:69
  267.1 11.5 %collective-permute-start.18 = (bf16[2,256,4096]{2,1,0:T(8,128)(2,1)}, bf16[2,256,4096]{2,1,0:T(8,128)(2,1)}, u32[]{:S(2)}, u32[]{:S(2)}) collective-permute-start(bf16[2,256,4096]{2,1,0:T(8,128)(2,1)} %get-tuple-element.105), channel_id=1, source_target_pairs={{0,8},{8,0},{1,9},{9,1},{2,10},{10,2},{3,11},{11,3},{4,12},{12,4},... | collective-permute-start | bytes 12582920 | tf_op jit(solution)/shard_map/ppermute | solution.py:69
  267.2 8.5 %collective-permute-start.19 = (bf16[2,256,1024]{2,1,0:T(8,128)(2,1)}, bf16[2,256,1024]{2,1,0:T(8,128)(2,1)S(1)}, u32[]{:S(2)}, u32[]{:S(2)}) collective-permute-start(bf16[2,256,1024]{2,1,0:T(8,128)(2,1)} %get-tuple-element.110), channel_id=1, source_target_pairs={{0,8},{8,0},{1,9},{9,1},{2,10},{10,2},{3,11},{11,3},{4,12},{12,4},... | collective-permute-start | bytes 3145736 | tf_op jit(solution)/shard_map/ppermute | solution.py:69
  278.4 117.0 %reduce-scatter.9.cloned.1.call-start = ((), (), s32[]{:S(2)}) async-start(), calls=%async_computation.8 | async-start | bytes 1310720 | tf_op jit(solution)/shard_map/reduce_scatter | solution.py:220
  282.8 57.4 %collective-permute-start.20 = (bf16[2,2,32,4096]{3,2,1,0:T(8,128)(2,1)S(1)}, bf16[2,2,32,4096]{3,2,1,0:T(8,128)(2,1)}, u32[]{:S(2)}, u32[]{:S(2)}) collective-permute-start(bf16[2,2,32,4096]{3,2,1,0:T(8,128)(2,1)S(1)} %get-tuple-element.185.refs_4_), channel_id=1, source_target_pairs={{0,1},{1,0},{16,17},{17,16},{2,3},{3,2},{18,19},{19,18},{4,5},{5,4... | collective-permute-start | bytes 3145736 | tf_op jit(solution)/shard_map/ppermute | solution.py:69
  283.1 57.1 %collective-permute-start.21 = (bf16[2,2,32,4096]{3,2,1,0:T(8,128)(2,1)S(1)}, bf16[2,2,32,4096]{3,2,1,0:T(8,128)(2,1)}, u32[]{:S(2)}, u32[]{:S(2)}) collective-permute-start(bf16[2,2,32,4096]{3,2,1,0:T(8,128)(2,1)S(1)} %get-tuple-element.184.refs_5_), channel_id=1, source_target_pairs={{0,16},{1,17},{16,0},{17,1},{2,18},{3,19},{18,2},{19,3},{4,20},{5,... | collective-permute-start | bytes 3145736 | tf_op jit(solution)/shard_map/ppermute | solution.py:69
  284.6 55.6 %collective-permute-start.22 = (bf16[2,2,32,4096]{3,2,1,0:T(8,128)(2,1)S(1)}, bf16[2,2,32,4096]{3,2,1,0:T(8,128)(2,1)}, u32[]{:S(2)}, u32[]{:S(2)}) collective-permute-start(bf16[2,2,32,4096]{3,2,1,0:T(8,128)(2,1)S(1)} %get-tuple-element.183.refs_6_), channel_id=1, source_target_pairs={{0,17},{1,16},{16,1},{17,0},{2,19},{3,18},{18,3},{19,2},{4,21},{5,... | collective-permute-start | bytes 3145736 | tf_op jit(solution)/shard_map/ppermute | solution.py:69
  340.2 5.9 %collective-permute-start.23 = (bf16[3,512,1024]{2,1,0:T(8,128)(2,1)}, bf16[3,512,1024]{2,1,0:T(8,128)(2,1)S(1)}, u32[]{:S(2)}, u32[]{:S(2)}) collective-permute-start(bf16[3,512,1024]{2,1,0:T(8,128)(2,1)} %get-tuple-element.116), channel_id=1, source_target_pairs={{0,8},{8,0},{1,9},{9,1},{2,10},{10,2},{3,11},{11,3},{4,12},{12,4},... | collective-permute-start | bytes 9437192 | tf_op jit(solution)/shard_map/ppermute | solution.py:69
  345.8 73.4 %reduce-scatter.11.cloned.1.call-start = ((), (), s32[]{:S(2)}) async-start(), calls=%async_computation.9 | async-start | bytes 983040 | tf_op jit(solution)/shard_map/reduce_scatter | solution.py:220
  351.4 37.3 %collective-permute-start.24 = (bf16[3,2,2,32,1024]{4,3,2,1,0:T(8,128)(2,1)S(1)}, bf16[3,2,2,32,1024]{4,3,2,1,0:T(8,128)(2,1)}, u32[]{:S(2)}, u32[]{:S(2)}) collective-permute-start(bf16[3,2,2,32,1024]{4,3,2,1,0:T(8,128)(2,1)S(1)} %get-tuple-element.188.refs_8_), channel_id=1, source_target_pairs={{0,1},{1,0},{16,17},{17,16},{2,3},{3,2},{18,19},{19,18},{4,5},{5,4... | collective-permute-start | bytes 2359304 | tf_op jit(solution)/shard_map/ppermute | solution.py:69
  351.7 37.1 %collective-permute-start.25 = (bf16[3,2,2,32,1024]{4,3,2,1,0:T(8,128)(2,1)S(1)}, bf16[3,2,2,32,1024]{4,3,2,1,0:T(8,128)(2,1)}, u32[]{:S(2)}, u32[]{:S(2)}) collective-permute-start(bf16[3,2,2,32,1024]{4,3,2,1,0:T(8,128)(2,1)S(1)} %get-tuple-element.187.refs_9_), channel_id=1, source_target_pairs={{0,16},{1,17},{16,0},{17,1},{2,18},{3,19},{18,2},{19,3},{4,20},{5,... | collective-permute-start | bytes 2359304 | tf_op jit(solution)/shard_map/ppermute | solution.py:69
  353.2 35.6 %collective-permute-start.26 = (bf16[3,2,2,32,1024]{4,3,2,1,0:T(8,128)(2,1)S(1)}, bf16[3,2,2,32,1024]{4,3,2,1,0:T(8,128)(2,1)}, u32[]{:S(2)}, u32[]{:S(2)}) collective-permute-start(bf16[3,2,2,32,1024]{4,3,2,1,0:T(8,128)(2,1)S(1)} %get-tuple-element.186.refs_10_), channel_id=1, source_target_pairs={{0,17},{1,16},{16,1},{17,0},{2,19},{3,18},{18,3},{19,2},{4,21},{5,... | collective-permute-start | bytes 2359304 | tf_op jit(solution)/shard_map/ppermute | solution.py:69
  372.1 19.7 %collective-permute-start.27 = (f32[2,2,2,2,384]{4,3,2,1,0:T(2,128)S(1)}, f32[2,2,2,2,384]{4,3,2,1,0:T(2,128)S(1)}, u32[]{:S(2)}, u32[]{:S(2)}) collective-permute-start(f32[2,2,2,2,384]{4,3,2,1,0:T(2,128)S(1)} %dynamic-slice_bitcast_fusion.1.refs_1_), channel_id=1, source_target_pairs={{0,8},{8,0},{1,9},{9,1},{2,10},{10,2},{3,11},{11,3},{4,12},{12,4},... | collective-permute-start | bytes 73736 | tf_op jit(solution)/shard_map/ppermute | solution.py:69
  372.3 23.1 %collective-permute-start.34 = (bf16[2,32,2048]{2,1,0:T(8,128)(2,1)S(1)}, bf16[2,32,2048]{2,1,0:T(8,128)(2,1)S(1)}, u32[]{:S(2)}, u32[]{:S(2)}) collective-permute-start(bf16[2,32,2048]{2,1,0:T(8,128)(2,1)S(1)} %dynamic-slice_bitcast_fusion.refs_2_), channel_id=1, source_target_pairs={{0,16},{16,0},{1,17},{17,1},{2,18},{18,2},{3,19},{19,3},{4,20},{20... | collective-permute-start | bytes 786440 | tf_op jit(solution)/shard_map/ppermute | solution.py:69
  398.8 5.7 %collective-permute-start.33 = (f32[384]{0:T(512)S(1)}, f32[384]{0:T(512)S(1)}, u32[]{:S(2)}, u32[]{:S(2)}) collective-permute-start(f32[384]{0:T(512)S(1)} %add_add_fusion.1), channel_id=1, source_target_pairs={{0,6},{2,4},{4,2},{6,0},{1,7},{3,5},{5,3},{7,1},{8,14},{10,12},{12... | collective-permute-start | bytes 4616 | tf_op jit(solution)/shard_map/ppermute | solution.py:69
  (43 other events, 579.8 us)
Sparse Core Ops, SparseCore 0:
  11.5 110.7 all-gather.2
  125.3 77.2 all-gather.4
  204.8 25.7 reduce-scatter.4
  278.6 25.9 reduce-scatter.6
  346.0 26.0 reduce-scatter.8
  396.6 22.6 reduce-scatter.10
